TPU v7x, 32 devices: a whole 2x2x4 slice. The times are simulated.
32 devices in a mesh: blk: 8 (over z, x), rep: 4 (over y, core).
Axes of the slice: x: 2, y: 2, z: 4, core: 2. Of those that a mesh axis runs over, the one named last changes fastest.
Arguments:
- amplitudes: bfloat16 [256, 24576], P(None, ('blk', 'rep')), may hold values from -6 to 6
- panels: bfloat16 [1376, 192, 768], P(('blk', 'rep')), may hold values from -0.21875 to 0.21875
- panel_owner_index: int32 [1376, 1], P(('blk', 'rep')), may hold values from 0 to 7; in each aligned block of 43 rows (0 to 42, 43 to 85, ...) at most 11 rows name the same one
- panel_target_tile: int32 [1376], P(('blk', 'rep')), may hold values from 0 to 15
- panel_tile_mask: int32 [1376, 4], P(('blk', 'rep')), may hold values 0 or 1
- tile_sizes: int32 [128], replicated, may hold values from 64 to 192
- tile_irreps: int32 [128], replicated, may hold values from 0 to 1
- occ_energy: float32 [256], P('rep'), may hold values from -3 to -0.5
- vir_energy: float32 [24576], P('blk'), may hold values from 0.5 to 6
Outputs:
- doubles_update: bfloat16 [256, 24576], P('rep', 'blk')
Inputs may be any that keep to these rules, and one draw needn't show every extreme that they name: `panel_owner_index`: within the 43 rows of one device no index of blk is named more than 11 times, a bound that some block reaches.
All inputs are finite; a program needn't handle non-finite values. No bound on the sum of `panel_tile_mask` on one device may be relied on, other than what follows from the above.
Results may differ from a plain program's by a relative error of at most 0.0049.
Values may be sent and summed in bfloat16 or wider, within the bound.
No kernel may reach another device: no remote copies, remote signals or barrier semaphores. Data moves between devices by JAX's collectives and lax.ppermute only.
A program may use at most 128 MiB of HBM per device.

v0:
```python
import functools

import jax
import jax.numpy as jnp
from jax import lax
from jax.experimental import pallas as pl
from jax.experimental.pallas import tpu as pltpu
from jax.sharding import PartitionSpec as P

LANES = 128
COPY_PANELS = 11
SHARES = (4, 3, 3, 2)


def stage_factors(count):
    factors, rest = [], count
    while rest > 1:
        factor = min(4 if factors else 2, rest)
        factors.append(factor)
        rest //= factor
    return factors


def task_order(parts, stages):
    keys = [(part - 2.6, part, -1) for part in range(parts)]
    keys += [(part + 1.5 * stage, part, stage) for part in range(parts) for stage in range(stages)]
    return [(part, stage) for _, part, stage in sorted(keys)]


def whole(memory_space=pltpu.VMEM):
    return pl.BlockSpec(memory_space=memory_space)


def nbytes(*arrays):
    total = 0
    for a in arrays:
        size = jnp.dtype(a.dtype).itemsize
        for d in a.shape:
            size *= d
        total += size
    return total


def grant(*arrays):
    return pltpu.CompilerParams(vmem_limit_bytes=min(62 << 20, nbytes(*arrays) * 3 // 2 + (4 << 20)))


def half_rows(low, high):
    lane = lax.broadcasted_iota(jnp.int32, low.shape, low.ndim - 1)
    width = LANES // 2
    first = jnp.where(lane < width, low, pltpu.roll(high, width, high.ndim - 1))
    second = jnp.where(lane < width, pltpu.roll(low, width, low.ndim - 1), high)
    return first, second


def column_sum(pick, values):
    return jnp.sum(jnp.where(pick, values, 0.0), axis=1, keepdims=True)


def live_factors(owner, tile, mask, sizes, irreps, device, owned, depth):
    tiles, count = mask.shape
    width, total = depth // tiles, sizes.shape[-1]
    eye = lax.broadcasted_iota(jnp.int32, (count, count), 0) == lax.broadcasted_iota(
        jnp.int32, (count, count), 1
    )
    size_row = sizes.reshape(1, total).astype(jnp.float32)
    irrep_row = irreps.reshape(1, total).astype(jnp.float32)
    target_row = owner * owned + tile.reshape(1, count)
    target = column_sum(eye, target_row.astype(jnp.float32)).astype(jnp.int32)
    tile_index = lax.broadcasted_iota(jnp.int32, (count, total), 1)
    irrep_target = column_sum(tile_index == target, irrep_row)
    column = lax.broadcasted_iota(jnp.int32, (count, depth), 1)
    keep = None
    for j in range(tiles):
        source = tile_index[:1] == device * tiles + j
        masked = column_sum(eye, mask[j : j + 1, :].astype(jnp.float32))
        live = (masked != 0.0) & (irrep_target == column_sum(source, irrep_row))
        limit = jnp.where(live, column_sum(source, size_row), 0.0).astype(jnp.int32)
        inside = (column >= j * width) & (column < j * width + limit)
        keep = inside if keep is None else keep | inside
    return target_row, keep.astype(jnp.float32)


def partial_kernel(span, owned, tables, extra, *refs):
    amp, panels = refs[tables : tables + 2]
    outs = refs[tables + 2 + extra :]
    copied, (buffer, amp_here, sem, small) = outs[-4 - tables : -4], outs[-4:]
    rep_count, row_count, depth = amp.shape
    count = panels.shape[0]
    loads = [
        pltpu.make_async_copy(source, target, small.at[i])
        for i, (source, target) in enumerate(zip((*refs[:tables], amp), (*copied, amp_here)))
    ]
    for load in loads:
        load.start()
    first, rows = span
    copies = []
    for start in range(0, count, COPY_PANELS):
        piece = pl.ds(start, min(COPY_PANELS, count - start))
        copies.append(
            pltpu.make_async_copy(
                panels.at[piece, :, pl.ds(first, rows)], buffer.at[piece], sem.at[len(copies)]
            )
        )
        copies[-1].start()
    for load in loads:
        load.wait()

    rep_index = lax.axis_index("rep")
    amp_t = jnp.concatenate([amp_here[rep_index ^ k] for k in range(rep_count)], axis=0).T
    if tables > 1:
        device = lax.axis_index("blk") * rep_count + rep_index
        ids, factors, *outs = outs
        ids[...], factors[...] = live_factors(*[t[...] for t in copied], device, owned, depth)
    else:
        factors = copied[0]

    for copy in copies:
        copy.wait()
    halves = buffer.shape[1]
    factor = factors[...].astype(jnp.bfloat16)
    live_panels = buffer[...] * factor[:, None, None, :]
    product = jnp.dot(
        live_panels.reshape(count * halves * rows, depth),
        amp_t,
        preferred_element_type=jnp.float32,
    )
    product = product.reshape(count, halves, rows, rep_count * row_count)
    for pair in range(rep_count // 2):
        lanes = slice(pair * LANES, (pair + 1) * LANES)
        packed = half_rows(product[:, 0, :, lanes], product[:, 1, :, lanes])
        for side, value in enumerate(packed):
            outs[2 * pair + side][...] = value.astype(jnp.bfloat16)


def partials(tables, amp, panels, span, owned, after=None):
    count, halves, _, depth = panels.shape
    rep_count, row_count, _ = amp.shape
    rows = span[1]
    outs = []
    if len(tables) > 1:
        outs += [
            jax.ShapeDtypeStruct((1, count), jnp.int32),
            jax.ShapeDtypeStruct((count, depth), jnp.float32),
        ]
    heads = len(outs)
    outs += [jax.ShapeDtypeStruct((count, rows, LANES), jnp.bfloat16)] * rep_count
    extra = [] if after is None else [after]
    results = pl.pallas_call(
        functools.partial(partial_kernel, span, owned, len(tables), len(extra)),
        out_shape=outs,
        in_specs=[whole(pl.ANY)] * (len(tables) + 2 + len(extra)),
        out_specs=[whole()] * len(outs),
        scratch_shapes=[
            *[pltpu.VMEM(t.shape, t.dtype) for t in tables],
            pltpu.VMEM((count, halves, rows, depth), jnp.bfloat16),
            pltpu.VMEM(amp.shape, amp.dtype),
            pltpu.SemaphoreType.DMA((pl.cdiv(count, COPY_PANELS),)),
            pltpu.SemaphoreType.DMA((len(tables) + 1,)),
        ],
        compiler_params=pltpu.CompilerParams(
            vmem_limit_bytes=(62 << 20) if heads else (66 << 20) - nbytes(panels)
        ),
        cost_estimate=pl.CostEstimate(
            flops=2 * count * halves * rows * depth * rep_count * row_count,
            bytes_accessed=2 * count * halves * rows * (depth + rep_count * row_count),
            transcendentals=0,
        ),
        name="partials",
    )(*tables, amp, panels, *extra)
    return results[:heads], results[heads:]


def gather_kernel(count_ids, factor, *refs):
    ids, parts = refs[:count_ids], refs[count_ids : 2 * count_ids]
    outs, ladders, own, sem = refs[-factor - 4 : -4], refs[-4:-2], refs[-2], refs[-1]
    count = own.shape[0]
    rest, tiles = outs[0].shape[:2]
    load = pltpu.make_async_copy(parts[0], own, sem)
    load.start()
    for ladder in ladders:
        ladder[...] = jnp.zeros_like(ladder)

    def add(left, right):
        for s in range(count):
            rows = []
            for ladder, (index, part) in zip(ladders, (left, right)):
                place = index[0, s]
                rows.append((ladder, place, ladder[place] + part[s].astype(jnp.float32)))
            for ladder, place, value in rows:
                ladder[place] = value

    received = list(zip(ids[1:], parts[1:]))
    add(received[0], received[1])
    load.wait()
    add(received[2], (ids[0], own))
    digit = lax.axis_index("blk") % factor
    for k in range(factor):
        for z in range(rest):
            span = pl.ds((z * factor + (digit ^ k)) * tiles, tiles)
            outs[k][z] = (ladders[0][span] + ladders[1][span]).astype(outs[k].dtype)


def gather_tiles(ids, parts, blk_count, tiles, factor, after=None):
    _, rows, _ = parts[0].shape
    shape = (blk_count // factor, tiles, rows, LANES)
    outs = [jax.ShapeDtypeStruct(shape, jnp.bfloat16 if k else jnp.float32) for k in range(factor)]
    ladder = pltpu.VMEM((blk_count * tiles, rows, LANES), jnp.float32)
    extra = [] if after is None else [after]
    return pl.pallas_call(
        functools.partial(gather_kernel, len(ids), factor),
        out_shape=outs,
        in_specs=[whole(pltpu.SMEM)] * len(ids)
        + [whole(pl.ANY)]
        + [whole()] * (len(parts) - 1)
        + [whole(pl.ANY)] * len(extra),
        out_specs=[whole()] * factor,
        scratch_shapes=[ladder] * 2
        + [pltpu.VMEM(parts[0].shape, parts[0].dtype), pltpu.SemaphoreType.DMA],
        compiler_params=grant(*parts, *outs, ladder, ladder),
        cost_estimate=pl.CostEstimate(
            flops=blk_count * tiles * rows * LANES,
            bytes_accessed=8 * blk_count * tiles * rows * LANES,
            transcendentals=0,
        ),
        name="gather_tiles",
    )(*ids, *parts, *extra)


def merge_kernel(arrays, factor, stride, *refs):
    ins, outs = refs[:arrays], refs[-factor:]
    rest = outs[0].shape[0]
    digit = (lax.axis_index("blk") // stride) % factor
    for k in range(factor):
        for z in range(rest):
            owner = z * factor + (digit ^ k)
            total = ins[0][owner]
            for other in ins[1:]:
                total = total + other[owner].astype(jnp.float32)
            outs[k][z] = total.astype(outs[k].dtype)


def merge(arrays, factor, stride, after=None):
    owners, tiles, rows, _ = arrays[0].shape
    shape = (owners // factor, tiles, rows, LANES)
    outs = [jax.ShapeDtypeStruct(shape, jnp.bfloat16 if k else jnp.float32) for k in range(factor)]
    extra = [] if after is None else [after]
    return pl.pallas_call(
        functools.partial(merge_kernel, len(arrays), factor, stride),
        out_shape=outs,
        in_specs=[whole()] * len(arrays) + [whole(pl.ANY)] * len(extra),
        out_specs=[whole()] * factor,
        compiler_params=grant(*arrays, *outs),
        cost_estimate=pl.CostEstimate(
            flops=owners * tiles * rows * LANES,
            bytes_accessed=8 * owners * tiles * rows * LANES,
            transcendentals=0,
        ),
        name="merge",
    )(*arrays, *extra)


def finish_kernel(per_part, *refs):
    occ, vir, keep, out = refs[0], refs[1], refs[2], refs[-1]
    ins = refs[3:-1]
    tiles = ins[0].shape[0]
    totals = []
    for start in range(0, len(ins), per_part):
        total = ins[start][...]
        for other in ins[start + 1 : start + per_part]:
            total = total + other[...].astype(jnp.float32)
        totals.append(total)
    total = jnp.concatenate(totals, axis=1)
    half = tiles // 2
    first, second = half_rows(total[:half], total[half:])
    rows = jnp.stack([first, second], axis=1).reshape(-1, LANES)
    flipped = rows.T
    columns = rows.shape[0]
    row_count = out.shape[0]
    for side in range(2):
        lanes = slice(side * columns, (side + 1) * columns)
        value = flipped[side * row_count : (side + 1) * row_count]
        denominator = occ[...] - vir[:, lanes]
        kept = keep[:, lanes] != 0
        out[:, lanes] = jnp.where(kept, value / denominator, 0.0).astype(jnp.bfloat16)


def finish(occ, vir, keep, arrays, per_part):
    out = jax.ShapeDtypeStruct((occ.shape[0], vir.shape[1]), jnp.bfloat16)
    return pl.pallas_call(
        functools.partial(finish_kernel, per_part),
        out_shape=out,
        in_specs=[whole()] * (3 + len(arrays)),
        out_specs=whole(),
        compiler_params=grant(out, out, out, *arrays),
        name="finish",
    )(occ, vir, keep, *arrays)


def shards(
    amplitudes,
    panels,
    panel_owner_index,
    panel_target_tile,
    panel_tile_mask,
    tile_sizes,
    tile_irreps,
    occ_energy,
    vir_energy,
):
    blk_count = lax.axis_size("blk")
    rep_count = lax.axis_size("rep")
    blk_index = lax.axis_index("blk")
    count, width, depth = panels.shape
    tiles_here = depth // width
    owned = tiles_here * rep_count
    row_count = amplitudes.shape[0] // rep_count
    halves = LANES // row_count
    packed = width // halves
    factors = stage_factors(blk_count)

    amp = amplitudes.reshape(rep_count, row_count, depth)
    panels = panels.reshape(count, halves, packed, depth)
    tables = [
        panel_owner_index.T,
        panel_target_tile,
        panel_tile_mask.T,
        tile_sizes,
        tile_irreps,
    ]

    def swap_rep(value, k):
        return lax.ppermute(value, "rep", [(i, i ^ k) for i in range(rep_count)])

    def swap_blk(value, k):
        return lax.ppermute(value, "blk", [(i, i ^ k) for i in range(blk_count)])

    spans, first = [], 0
    for share in SHARES:
        rows = packed * share // sum(SHARES)
        spans.append((first, rows))
        first += rows

    last, ids, strides = None, None, [1]
    for factor in factors:
        strides.append(strides[-1] * factor)
    pending = [None] * len(spans)
    for part, stage in task_order(len(spans), len(factors)):
        if stage < 0:
            heads, (own, *others) = partials(tables, amp, panels, spans[part], owned, last)
            last = own
        elif stage == 0:
            arrays = gather_tiles(ids, pending[part], blk_count, owned, factors[0], last)
            last = arrays[0]
        else:
            arrays = merge(pending[part], factors[stage], strides[stage], last)
            last = arrays[0]
        if stage < 0:
            swapped = [swap_rep(others[k - 1], k) for k in range(1, rep_count)]
            pending[part] = [own, *swapped]
            if heads:
                tables = heads[1:]
                ids = [heads[0]] + [swap_rep(heads[0], k) for k in range(1, rep_count)]
        else:
            stride = strides[stage]
            swapped = [swap_blk(arrays[k], k * stride) for k in range(1, factors[stage])]
            pending[part] = [arrays[0], *swapped]
    collected = [value[0] for part in pending for value in part]

    sizes_owned = lax.dynamic_slice_in_dim(tile_sizes, blk_index * owned, owned, 0)
    in_tile = jnp.arange(width, dtype=jnp.int32)
    keep = (in_tile[None, :] < sizes_owned[:, None]).astype(jnp.int32).reshape(1, owned * width)
    return finish(
        occ_energy[:, None], vir_energy[None, :], keep, collected, len(pending[0])
    )


def solution(mesh):
    return jax.shard_map(
        shards,
        mesh=mesh,
        in_specs=(
            P(None, ("blk", "rep")),
            P(("blk", "rep"), None, None),
            P(("blk", "rep"), None),
            P(("blk", "rep")),
            P(("blk", "rep"), None),
            P(),
            P(),
            P("rep"),
            P("blk"),
        ),
        out_specs=P("rep", "blk"),
        check_vma=False,
    )
```

profile of v0, /device:TPU:0, one launch (start us, length us, event | category | flops | bytes accessed | tf_op | source)
XLA Modules:
  0.0 111.6 jit_solution(18164520208260796100)
XLA Ops:
  0.0 4.9 %partials.4 = (s32[1,43]{1,0:T(1,128)}, f32[43,768]{1,0:T(8,128)}, bf16[43,32,128]{2,1,0:T(8,128)(2,1)}, bf16[43,32,128]{2,1,0:T(8,128)(2,1)}, bf16[43,32,128]{2...) custom-call(s32[1,43]{1,0:T(1,128)} %bitcast.48, s32[43]{0:T(128)} %refs_1_.1, s32[4,43]{1,0:T(4,128)} %bitcast.47, s32[128]{0:T(128)} %refs_3_.1, ...), custom_call_target="tpu_custom_call" | custom-call | flops 1082130432 | bytes 5636096 | tf_op jit(solution)/shard_map/partials/pallas_call | solution.py:149
  4.9 0.6 collective-permute-start.3
  5.5 2.6 %collective-permute-start.4 = (bf16[43,32,128]{2,1,0:T(8,128)(2,1)}, bf16[43,32,128]{2,1,0:T(8,128)(2,1)S(1)}, u32[]{:S(2)}, u32[]{:S(2)}) collective-permute-start(bf16[43,32,128]{2,1,0:T(8,128)(2,1)} %get-tuple-element.50), channel_id=1, source_target_pairs={{0,2},{1,3},{2,0},{3,1},{4,6},{5,7},{6,4},{7,5},{8,10},{9,11},{10,... | collective-permute-start | bytes 1056776 | tf_op jit(solution)/shard_map/ppermute | solution.py:333
  8.1 0.0 collective-permute-start.5
  8.1 0.2 collective-permute-start
  8.3 1.9 %collective-permute-start.1 = (s32[1,43]{1,0:T(1,128)}, s32[1,43]{1,0:T(1,128)S(1)}, u32[]{:S(2)}, u32[]{:S(2)}) collective-permute-start(s32[1,43]{1,0:T(1,128)} %get-tuple-element.47.refs_0_), channel_id=1, source_target_pairs={{0,2},{1,3},{2,0},{3,1},{4,6},{5,7},{6,4},{7,5},{8,10},{9,11},{10,... | collective-permute-start | bytes 524 | tf_op jit(solution)/shard_map/ppermute | solution.py:333
  10.2 4.2 %partials.5 = (bf16[43,24,128]{2,1,0:T(8,128)(2,1)}, bf16[43,24,128]{2,1,0:T(8,128)(2,1)}, bf16[43,24,128]{2,1,0:T(8,128)(2,1)}, bf16[43,24,128]{2,1,0:T(8,128)(2,1)}) custom-call(f32[43,768]{1,0:T(8,128)} %get-tuple-element.52.refs_0_, bf16[4,64,768]{2,1,0:T(8,128)(2,1)} %bitcast.44, bf16[43,2,96,768]{3,2,1,0:T(8,128)(2,1)} %bitcast.40, ...), custom_call_target="tpu_custom_call" | custom-call | flops 811597824 | bytes 4227072 | tf_op jit(solution)/shard_map/partials/pallas_call | solution.py:149
  14.5 0.0 collective-permute-done.refs_1_
  14.5 0.1 collective-permute-start.2
  14.6 10.1 %collective-permute-done.1.refs_2_ = s32[1,43]{1,0:T(1,128)S(1)} collective-permute-done((s32[1,43]{1,0:T(1,128)}, s32[1,43]{1,0:T(1,128)S(1)}, u32[]{:S(2)}, u32[]{:S(2)}) %collective-permute-start.1) | collective-permute-done | bytes 204 | tf_op jit(solution)/shard_map/ppermute | solution.py:333
  24.7 4.2 %partials.6 = (bf16[43,24,128]{2,1,0:T(8,128)(2,1)}, bf16[43,24,128]{2,1,0:T(8,128)(2,1)}, bf16[43,24,128]{2,1,0:T(8,128)(2,1)}, bf16[43,24,128]{2,1,0:T(8,128)(2,1)}) custom-call(f32[43,768]{1,0:T(8,128)} %get-tuple-element.52.refs_0_, bf16[4,64,768]{2,1,0:T(8,128)(2,1)} %bitcast.45, bf16[43,2,96,768]{3,2,1,0:T(8,128)(2,1)} %bitcast.41, ...), custom_call_target="tpu_custom_call" | custom-call | flops 811597824 | bytes 4227072 | tf_op jit(solution)/shard_map/partials/pallas_call | solution.py:149
  28.9 0.0 collective-permute-done.3.refs_5_
  29.0 0.0 collective-permute-done.4.refs_6_
  29.0 0.9 copy-done.3
  29.9 1.7 %gather_tiles.4 = (f32[4,16,32,128]{3,2,1,0:T(8,128)S(1)}, bf16[4,16,32,128]{3,2,1,0:T(8,128)(2,1)S(1)}) custom-call(s32[1,43]{1,0:T(1,128)S(1)} %copy-done.8, s32[1,43]{1,0:T(1,128)S(1)} %collective-permute-done.refs_1_, s32[1,43]{1,0:T(1,128)S(1)} %collective-permute-done.1.refs_2_, s32[1,43]{1,0:T(1,128)S(1)} %collective-permute-done.2.refs_3_, ...), custom_call_target="tpu_custom_call" | custom-call | flops 524288 | bytes 4194304 | tf_op jit(solution)/shard_map/gather_tiles/pallas_call | solution.py:210
  31.6 1.0 copy-done
  32.6 1.8 %collective-permute-start.6 = (bf16[4,16,32,128]{3,2,1,0:T(8,128)(2,1)S(1)}, bf16[4,16,32,128]{3,2,1,0:T(8,128)(2,1)S(1)}, u32[]{:S(2)}, u32[]{:S(2)}) collective-permute-start(bf16[4,16,32,128]{3,2,1,0:T(8,128)(2,1)S(1)} %get-tuple-element.56), channel_id=1, source_target_pairs={{0,4},{4,0},{8,12},{12,8},{16,20},{20,16},{24,28},{28,24},{1,5},{5... | collective-permute-start | bytes 1572872 | tf_op jit(solution)/shard_map/ppermute | solution.py:336
  34.4 1.5 %collective-permute-start.8 = (bf16[43,24,128]{2,1,0:T(8,128)(2,1)S(1)}, bf16[43,24,128]{2,1,0:T(8,128)(2,1)S(1)}, u32[]{:S(2)}, u32[]{:S(2)}) collective-permute-start(bf16[43,24,128]{2,1,0:T(8,128)(2,1)S(1)} %copy-done.13), channel_id=1, source_target_pairs={{0,2},{1,3},{2,0},{3,1},{4,6},{5,7},{6,4},{7,5},{8,10},{9,11},{10,... | collective-permute-start | bytes 792584 | tf_op jit(solution)/shard_map/ppermute | solution.py:333
  35.9 0.0 collective-permute-start.9
  36.0 0.6 collective-permute-start.14
  36.5 0.0 collective-permute-done.7.refs_5_
  36.5 1.5 %collective-permute-start.15 = (bf16[43,24,128]{2,1,0:T(8,128)(2,1)}, bf16[43,24,128]{2,1,0:T(8,128)(2,1)S(1)}, u32[]{:S(2)}, u32[]{:S(2)}) collective-permute-start(bf16[43,24,128]{2,1,0:T(8,128)(2,1)} %get-tuple-element.68), channel_id=1, source_target_pairs={{0,2},{1,3},{2,0},{3,1},{4,6},{5,7},{6,4},{7,5},{8,10},{9,11},{10,... | collective-permute-start | bytes 792584 | tf_op jit(solution)/shard_map/ppermute | solution.py:333
  38.1 3.4 %partials.7 = (bf16[43,16,128]{2,1,0:T(8,128)(2,1)}, bf16[43,16,128]{2,1,0:T(8,128)(2,1)}, bf16[43,16,128]{2,1,0:T(8,128)(2,1)}, bf16[43,16,128]{2,1,0:T(8,128)(2,1)}) custom-call(f32[43,768]{1,0:T(8,128)} %get-tuple-element.52.refs_0_, bf16[4,64,768]{2,1,0:T(8,128)(2,1)} %bitcast.46, bf16[43,2,96,768]{3,2,1,0:T(8,128)(2,1)} %bitcast.42, ...), custom_call_target="tpu_custom_call" | custom-call | flops 541065216 | bytes 2818048 | tf_op jit(solution)/shard_map/partials/pallas_call | solution.py:149
  41.5 2.1 %collective-permute-done.8.refs_6_ = bf16[43,24,128]{2,1,0:T(8,128)(2,1)S(1)} collective-permute-done((bf16[43,24,128]{2,1,0:T(8,128)(2,1)S(1)}, bf16[43,24,128]{2,1,0:T(8,128)(2,1)S(1)}, u32[]{:S(2)}, u32[]{:S(2)}) %collective-permute-start.8) | collective-permute-done | bytes 264224 | tf_op jit(solution)/shard_map/ppermute | solution.py:333
  43.6 4.7 %collective-permute-done.9.refs_7_ = bf16[43,24,128]{2,1,0:T(8,128)(2,1)S(1)} collective-permute-done((bf16[43,24,128]{2,1,0:T(8,128)(2,1)S(1)}, bf16[43,24,128]{2,1,0:T(8,128)(2,1)S(1)}, u32[]{:S(2)}, u32[]{:S(2)}) %collective-permute-start.9) | collective-permute-done | bytes 264224 | tf_op jit(solution)/shard_map/ppermute | solution.py:333
  48.3 0.9 copy-done.6
  49.2 1.4 %gather_tiles.5 = (f32[4,16,24,128]{3,2,1,0:T(8,128)S(1)}, bf16[4,16,24,128]{3,2,1,0:T(8,128)(2,1)S(1)}) custom-call(s32[1,43]{1,0:T(1,128)S(1)} %copy-done.8, s32[1,43]{1,0:T(1,128)S(1)} %collective-permute-done.refs_1_, s32[1,43]{1,0:T(1,128)S(1)} %collective-permute-done.1.refs_2_, s32[1,43]{1,0:T(1,128)S(1)} %collective-permute-done.2.refs_3_, ...), custom_call_target="tpu_custom_call" | custom-call | flops 393216 | bytes 3145728 | tf_op jit(solution)/shard_map/gather_tiles/pallas_call | solution.py:210
  50.6 0.6 collective-permute-start.13
  51.2 1.6 %collective-permute-start.16 = (bf16[43,24,128]{2,1,0:T(8,128)(2,1)S(1)}, bf16[43,24,128]{2,1,0:T(8,128)(2,1)S(1)}, u32[]{:S(2)}, u32[]{:S(2)}) collective-permute-start(bf16[43,24,128]{2,1,0:T(8,128)(2,1)S(1)} %copy-done.11), channel_id=1, source_target_pairs={{0,3},{1,2},{2,1},{3,0},{4,7},{5,6},{6,5},{7,4},{8,11},{9,10},{10,... | collective-permute-start | bytes 792584 | tf_op jit(solution)/shard_map/ppermute | solution.py:333
  52.8 1.4 %collective-permute-done.15.refs_6_ = bf16[43,24,128]{2,1,0:T(8,128)(2,1)S(1)} collective-permute-done((bf16[43,24,128]{2,1,0:T(8,128)(2,1)}, bf16[43,24,128]{2,1,0:T(8,128)(2,1)S(1)}, u32[]{:S(2)}, u32[]{:S(2)}) %collective-permute-start.15) | collective-permute-done | bytes 264224 | tf_op jit(solution)/shard_map/ppermute | solution.py:333
  54.2 2.0 %collective-permute-start.22 = (bf16[43,16,128]{2,1,0:T(8,128)(2,1)}, bf16[43,16,128]{2,1,0:T(8,128)(2,1)S(1)}, u32[]{:S(2)}, u32[]{:S(2)}) collective-permute-start(bf16[43,16,128]{2,1,0:T(8,128)(2,1)} %get-tuple-element.77), channel_id=1, source_target_pairs={{0,2},{1,3},{2,0},{3,1},{4,6},{5,7},{6,4},{7,5},{8,10},{9,11},{10,... | collective-permute-start | bytes 528392 | tf_op jit(solution)/shard_map/ppermute | solution.py:333
  56.3 0.1 merge.4
  56.4 3.2 %collective-permute-done.16.refs_7_ = bf16[43,24,128]{2,1,0:T(8,128)(2,1)S(1)} collective-permute-done((bf16[43,24,128]{2,1,0:T(8,128)(2,1)S(1)}, bf16[43,24,128]{2,1,0:T(8,128)(2,1)S(1)}, u32[]{:S(2)}, u32[]{:S(2)}) %collective-permute-start.16) | collective-permute-done | bytes 264224 | tf_op jit(solution)/shard_map/ppermute | solution.py:333
  59.6 1.4 %gather_tiles.6 = (f32[4,16,24,128]{3,2,1,0:T(8,128)S(1)}, bf16[4,16,24,128]{3,2,1,0:T(8,128)(2,1)S(1)}) custom-call(s32[1,43]{1,0:T(1,128)S(1)} %copy-done.8, s32[1,43]{1,0:T(1,128)S(1)} %collective-permute-done.refs_1_, s32[1,43]{1,0:T(1,128)S(1)} %collective-permute-done.1.refs_2_, s32[1,43]{1,0:T(1,128)S(1)} %collective-permute-done.2.refs_3_, ...), custom_call_target="tpu_custom_call" | custom-call | flops 393216 | bytes 3145728 | tf_op jit(solution)/shard_map/gather_tiles/pallas_call | solution.py:210
  61.0 1.6 %collective-permute-start.20 = (bf16[4,16,24,128]{3,2,1,0:T(8,128)(2,1)S(1)}, bf16[4,16,24,128]{3,2,1,0:T(8,128)(2,1)S(1)}, u32[]{:S(2)}, u32[]{:S(2)}) collective-permute-start(bf16[4,16,24,128]{3,2,1,0:T(8,128)(2,1)S(1)} %get-tuple-element.75), channel_id=1, source_target_pairs={{0,4},{4,0},{8,12},{12,8},{16,20},{20,16},{24,28},{28,24},{1,5},{5... | collective-permute-start | bytes 1179656 | tf_op jit(solution)/shard_map/ppermute | solution.py:336
  62.5 0.1 merge.5
  62.6 1.5 %collective-permute-done.22.refs_6_ = bf16[43,16,128]{2,1,0:T(8,128)(2,1)S(1)} collective-permute-done((bf16[43,16,128]{2,1,0:T(8,128)(2,1)}, bf16[43,16,128]{2,1,0:T(8,128)(2,1)S(1)}, u32[]{:S(2)}, u32[]{:S(2)}) %collective-permute-start.22) | collective-permute-done | bytes 176160 | tf_op jit(solution)/shard_map/ppermute | solution.py:333
  64.1 2.7 %collective-permute-done.23.refs_7_ = bf16[43,16,128]{2,1,0:T(8,128)(2,1)S(1)} collective-permute-done((bf16[43,16,128]{2,1,0:T(8,128)(2,1)}, bf16[43,16,128]{2,1,0:T(8,128)(2,1)S(1)}, u32[]{:S(2)}, u32[]{:S(2)}) %collective-permute-start.23) | collective-permute-done | bytes 176160 | tf_op jit(solution)/shard_map/ppermute | solution.py:333
  66.9 1.4 %gather_tiles.7 = (f32[4,16,16,128]{3,2,1,0:T(8,128)S(1)}, bf16[4,16,16,128]{3,2,1,0:T(8,128)(2,1)S(1)}) custom-call(s32[1,43]{1,0:T(1,128)S(1)} %copy-done.8, s32[1,43]{1,0:T(1,128)S(1)} %collective-permute-done.refs_1_, s32[1,43]{1,0:T(1,128)S(1)} %collective-permute-done.1.refs_2_, s32[1,43]{1,0:T(1,128)S(1)} %collective-permute-done.2.refs_3_, ...), custom_call_target="tpu_custom_call" | custom-call | flops 262144 | bytes 2097152 | tf_op jit(solution)/shard_map/gather_tiles/pallas_call | solution.py:210
  68.3 1.4 %collective-permute-start.27 = (bf16[4,16,16,128]{3,2,1,0:T(8,128)(2,1)S(1)}, bf16[4,16,16,128]{3,2,1,0:T(8,128)(2,1)S(1)}, u32[]{:S(2)}, u32[]{:S(2)}) collective-permute-start(bf16[4,16,16,128]{3,2,1,0:T(8,128)(2,1)S(1)} %get-tuple-element.84), channel_id=1, source_target_pairs={{0,4},{4,0},{8,12},{12,8},{16,20},{20,16},{24,28},{28,24},{1,5},{5... | collective-permute-start | bytes 786440 | tf_op jit(solution)/shard_map/ppermute | solution.py:336
  69.8 1.6 %collective-permute-start.17 = (bf16[1,16,24,128]{3,2,1,0:T(8,128)(2,1)S(1)}, bf16[1,16,24,128]{3,2,1,0:T(8,128)(2,1)S(1)}, u32[]{:S(2)}, u32[]{:S(2)}) collective-permute-start(bf16[1,16,24,128]{3,2,1,0:T(8,128)(2,1)S(1)} %get-tuple-element.72), channel_id=1, source_target_pairs={{0,8},{4,12},{8,0},{12,4},{16,24},{20,28},{24,16},{28,20},{1,9},{5... | collective-permute-start | bytes 294920 | tf_op jit(solution)/shard_map/ppermute | solution.py:336
  71.3 2.6 %collective-permute-start.18 = (bf16[1,16,24,128]{3,2,1,0:T(8,128)(2,1)S(1)}, bf16[1,16,24,128]{3,2,1,0:T(8,128)(2,1)S(1)}, u32[]{:S(2)}, u32[]{:S(2)}) collective-permute-start(bf16[1,16,24,128]{3,2,1,0:T(8,128)(2,1)S(1)} %get-tuple-element.73), channel_id=1, source_target_pairs={{0,16},{4,20},{8,24},{12,28},{16,0},{20,4},{24,8},{28,12},{1,17},{... | collective-permute-start | bytes 294920 | tf_op jit(solution)/shard_map/ppermute | solution.py:336
  73.9 0.4 collective-permute-start.10
  74.3 0.6 collective-permute-done.17
  75.0 3.2 %collective-permute-start.11 = (bf16[1,16,32,128]{3,2,1,0:T(8,128)(2,1)S(1)}, bf16[1,16,32,128]{3,2,1,0:T(8,128)(2,1)S(1)}, u32[]{:S(2)}, u32[]{:S(2)}) collective-permute-start(bf16[1,16,32,128]{3,2,1,0:T(8,128)(2,1)S(1)} %get-tuple-element.64), channel_id=1, source_target_pairs={{0,16},{4,20},{8,24},{12,28},{16,0},{20,4},{24,8},{28,12},{1,17},{... | collective-permute-start | bytes 393224 | tf_op jit(solution)/shard_map/ppermute | solution.py:336
  78.2 0.4 collective-permute-done.27.refs_1_
  78.6 3.6 %collective-permute-start.12 = (bf16[1,16,32,128]{3,2,1,0:T(8,128)(2,1)S(1)}, bf16[1,16,32,128]{3,2,1,0:T(8,128)(2,1)S(1)}, u32[]{:S(2)}, u32[]{:S(2)}) collective-permute-start(bf16[1,16,32,128]{3,2,1,0:T(8,128)(2,1)S(1)} %get-tuple-element.65), channel_id=1, source_target_pairs={{0,24},{4,28},{8,16},{12,20},{16,8},{20,12},{24,0},{28,4},{1,25},{... | collective-permute-start | bytes 393224 | tf_op jit(solution)/shard_map/ppermute | solution.py:336
  82.1 0.3 collective-permute-start.19
  82.4 0.1 merge.6
  82.5 0.1 merge.7
  82.6 0.4 collective-permute-start.28
  82.9 0.1 dynamic_slice.3
  83.0 7.2 %collective-permute-done.19 = bf16[1,16,24,128]{3,2,1,0:T(8,128)(2,1)S(1)} collective-permute-done((bf16[1,16,24,128]{3,2,1,0:T(8,128)(2,1)S(1)}, bf16[1,16,24,128]{3,2,1,0:T(8,128)(2,1)S(1)}, u32[]{:S(2)}, u32[]{:S(2)}) %collective-permute-start.19) | collective-permute-done | bytes 98336 | tf_op jit(solution)/shard_map/ppermute | solution.py:336
  90.2 7.2 %collective-permute-start.29 = (bf16[1,16,16,128]{3,2,1,0:T(8,128)(2,1)S(1)}, bf16[1,16,16,128]{3,2,1,0:T(8,128)(2,1)S(1)}, u32[]{:S(2)}, u32[]{:S(2)}) collective-permute-start(bf16[1,16,16,128]{3,2,1,0:T(8,128)(2,1)S(1)} %get-tuple-element.87), channel_id=1, source_target_pairs={{0,16},{4,20},{8,24},{12,28},{16,0},{20,4},{24,8},{28,12},{1,17},{... | collective-permute-start | bytes 196616 | tf_op jit(solution)/shard_map/ppermute | solution.py:336
  97.4 0.4 collective-permute-start.30
  97.8 0.1 collective-permute-start.24
  98.0 3.8 %collective-permute-start.25 = (bf16[1,16,24,128]{3,2,1,0:T(8,128)(2,1)S(1)}, bf16[1,16,24,128]{3,2,1,0:T(8,128)(2,1)S(1)}, u32[]{:S(2)}, u32[]{:S(2)}) collective-permute-start(bf16[1,16,24,128]{3,2,1,0:T(8,128)(2,1)S(1)} %get-tuple-element.82), channel_id=1, source_target_pairs={{0,16},{4,20},{8,24},{12,28},{16,0},{20,4},{24,8},{28,12},{1,17},{... | collective-permute-start | bytes 294920 | tf_op jit(solution)/shard_map/ppermute | solution.py:336
  101.8 0.4 collective-permute-start.26
  102.2 0.1 fusion
  102.3 0.1 reshape.37.refs_2_
  102.4 0.1 copy.10.refs_0_
  102.5 1.8 %collective-permute-done.30 = bf16[1,16,16,128]{3,2,1,0:T(8,128)(2,1)S(1)} collective-permute-done((bf16[1,16,16,128]{3,2,1,0:T(8,128)(2,1)S(1)}, bf16[1,16,16,128]{3,2,1,0:T(8,128)(2,1)S(1)}, u32[]{:S(2)}, u32[]{:S(2)}) %collective-permute-start.30) | collective-permute-done | bytes 65568 | tf_op jit(solution)/shard_map/ppermute | solution.py:336
  104.2 6.0 %collective-permute-done.25 = bf16[1,16,24,128]{3,2,1,0:T(8,128)(2,1)S(1)} collective-permute-done((bf16[1,16,24,128]{3,2,1,0:T(8,128)(2,1)S(1)}, bf16[1,16,24,128]{3,2,1,0:T(8,128)(2,1)S(1)}, u32[]{:S(2)}, u32[]{:S(2)}) %collective-permute-start.25) | collective-permute-done | bytes 98336 | tf_op jit(solution)/shard_map/ppermute | solution.py:336
  110.2 1.4 %finish.1 = bf16[64,3072]{1,0:T(8,128)(2,1)} custom-call(f32[64,1]{1,0:T(8,128)S(1)} %copy.10.refs_0_, f32[1,3072]{1,0:T(1,128)S(1)} %bitcast.38, s32[1,3072]{1,0:T(1,128)S(1)} %reshape.37.refs_2_, f32[16,32,128]{2,1,0:T(8,128)S(1)} %bitcast.22, bf16[16,32,128]{2,1,0:T(8,128)(2,1)S(1)} %bitcast.25, bf16[16,32,128]{2,1,0:T(8,128)(2,1)S(1)} %bitcast.26, ...), custom_call_target="tpu_custom_call" | custom-call | tf_op jit(solution)/shard_map/finish/pallas_call | solution.py:290
  (43 shorter events, 0.1 us)
Async XLA Ops:
  4.9 9.5 %copy-start.8 = (s32[1,43]{1,0:T(1,128)S(1)}, s32[1,43]{1,0:T(1,128)}, u32[]{:S(2)}) copy-start(s32[1,43]{1,0:T(1,128)} %get-tuple-element.47.refs_0_) | copy-start | bytes 520
  4.9 24.0 %collective-permute-start.3 = (bf16[43,32,128]{2,1,0:T(8,128)(2,1)}, bf16[43,32,128]{2,1,0:T(8,128)(2,1)S(1)}, u32[]{:S(2)}, u32[]{:S(2)}) collective-permute-start(bf16[43,32,128]{2,1,0:T(8,128)(2,1)} %get-tuple-element.49), channel_id=1, source_target_pairs={{0,1},{1,0},{2,3},{3,2},{4,5},{5,4},{6,7},{7,6},{8,9},{9,8},{10,11... | collective-permute-start | bytes 1056776 | tf_op jit(solution)/shard_map/ppermute | solution.py:333
  5.5 23.5 %collective-permute-start.4 = (bf16[43,32,128]{2,1,0:T(8,128)(2,1)}, bf16[43,32,128]{2,1,0:T(8,128)(2,1)S(1)}, u32[]{:S(2)}, u32[]{:S(2)}) collective-permute-start(bf16[43,32,128]{2,1,0:T(8,128)(2,1)} %get-tuple-element.50), channel_id=1, source_target_pairs={{0,2},{1,3},{2,0},{3,1},{4,6},{5,7},{6,4},{7,5},{8,10},{9,11},{10,... | collective-permute-start | bytes 1056776 | tf_op jit(solution)/shard_map/ppermute | solution.py:333
  8.1 20.9 %collective-permute-start.5 = (bf16[43,32,128]{2,1,0:T(8,128)(2,1)}, bf16[43,32,128]{2,1,0:T(8,128)(2,1)S(1)}, u32[]{:S(2)}, u32[]{:S(2)}) collective-permute-start(bf16[43,32,128]{2,1,0:T(8,128)(2,1)} %get-tuple-element.51), channel_id=1, source_target_pairs={{0,3},{1,2},{2,1},{3,0},{4,7},{5,6},{6,5},{7,4},{8,11},{9,10},{10,... | collective-permute-start | bytes 1056776 | tf_op jit(solution)/shard_map/ppermute | solution.py:333
  8.1 6.3 %collective-permute-start = (s32[1,43]{1,0:T(1,128)}, s32[1,43]{1,0:T(1,128)S(1)}, u32[]{:S(2)}, u32[]{:S(2)}) collective-permute-start(s32[1,43]{1,0:T(1,128)} %get-tuple-element.47.refs_0_), channel_id=1, source_target_pairs={{0,1},{1,0},{2,3},{3,2},{4,5},{5,4},{6,7},{7,6},{8,9},{9,8},{10,11... | collective-permute-start | bytes 524 | tf_op jit(solution)/shard_map/ppermute | solution.py:333
  8.3 16.4 %collective-permute-start.1 = (s32[1,43]{1,0:T(1,128)}, s32[1,43]{1,0:T(1,128)S(1)}, u32[]{:S(2)}, u32[]{:S(2)}) collective-permute-start(s32[1,43]{1,0:T(1,128)} %get-tuple-element.47.refs_0_), channel_id=1, source_target_pairs={{0,2},{1,3},{2,0},{3,1},{4,6},{5,7},{6,4},{7,5},{8,10},{9,11},{10,... | collective-permute-start | bytes 524 | tf_op jit(solution)/shard_map/ppermute | solution.py:333
  10.2 18.8 %copy-start.2 = (bf16[43,32,128]{2,1,0:T(8,128)(2,1)S(1)}, bf16[43,32,128]{2,1,0:T(8,128)(2,1)}, u32[]{:S(2)}) copy-start(bf16[43,32,128]{2,1,0:T(8,128)(2,1)} %get-tuple-element.48.refs_3_.refs_4_) | copy-start | bytes 1056772
  14.4 19.9 %copy-start.13 = (bf16[43,24,128]{2,1,0:T(8,128)(2,1)S(1)}, bf16[43,24,128]{2,1,0:T(8,128)(2,1)}, u32[]{:S(2)}) copy-start(bf16[43,24,128]{2,1,0:T(8,128)(2,1)} %get-tuple-element.58) | copy-start | bytes 792580
  14.5 21.5 %copy-start.12 = (bf16[43,24,128]{2,1,0:T(8,128)(2,1)S(1)}, bf16[43,24,128]{2,1,0:T(8,128)(2,1)}, u32[]{:S(2)}) copy-start(bf16[43,24,128]{2,1,0:T(8,128)(2,1)} %get-tuple-element.59) | copy-start | bytes 792580
  14.5 14.5 %collective-permute-start.2 = (s32[1,43]{1,0:T(1,128)S(1)}, s32[1,43]{1,0:T(1,128)S(1)}, u32[]{:S(2)}, u32[]{:S(2)}) collective-permute-start(s32[1,43]{1,0:T(1,128)S(1)} %copy-done.8), channel_id=1, source_target_pairs={{0,3},{1,2},{2,1},{3,0},{4,7},{5,6},{6,5},{7,4},{8,11},{9,10},{10,... | collective-permute-start | bytes 524 | tf_op jit(solution)/shard_map/ppermute | solution.py:333
  24.7 11.9 %collective-permute-start.7 = (bf16[43,24,128]{2,1,0:T(8,128)(2,1)}, bf16[43,24,128]{2,1,0:T(8,128)(2,1)S(1)}, u32[]{:S(2)}, u32[]{:S(2)}) collective-permute-start(bf16[43,24,128]{2,1,0:T(8,128)(2,1)} %get-tuple-element.57), channel_id=1, source_target_pairs={{0,1},{1,0},{2,3},{3,2},{4,5},{5,4},{6,7},{7,6},{8,9},{9,8},{10,11... | collective-permute-start | bytes 792584 | tf_op jit(solution)/shard_map/ppermute | solution.py:333
  24.7 23.6 %copy-start.5 = (bf16[43,24,128]{2,1,0:T(8,128)(2,1)S(1)}, bf16[43,24,128]{2,1,0:T(8,128)(2,1)}, u32[]{:S(2)}) copy-start(bf16[43,24,128]{2,1,0:T(8,128)(2,1)} %get-tuple-element.53.refs_3_.refs_4_) | copy-start | bytes 792580
  29.0 1.0 copy-start.3
  29.9 21.3 %copy-start.11 = (bf16[43,24,128]{2,1,0:T(8,128)(2,1)S(1)}, bf16[43,24,128]{2,1,0:T(8,128)(2,1)}, u32[]{:S(2)}) copy-start(bf16[43,24,128]{2,1,0:T(8,128)(2,1)} %get-tuple-element.69) | copy-start | bytes 792580
  29.9 29.6 %copy-start.4 = (bf16[43,24,128]{2,1,0:T(8,128)(2,1)S(1)}, bf16[43,24,128]{2,1,0:T(8,128)(2,1)}, u32[]{:S(2)}) copy-start(bf16[43,24,128]{2,1,0:T(8,128)(2,1)} %get-tuple-element.54.refs_8_.refs_4_) | copy-start | bytes 792580
  31.6 1.0 copy-start
  32.6 50.3 %copy-start.9 = (s32[128]{0:T(128)S(1)}, s32[128]{0:T(128)}, u32[]{:S(2)}) copy-start(s32[128]{0:T(128)} %refs_3_.1) | copy-start | bytes 1540
  32.6 69.8 %copy-start.10 = (f32[64]{0:T(128)S(1)}, f32[64]{0:T(128)}, u32[]{:S(2)}) copy-start(f32[64]{0:T(128)} %param.16) | copy-start | bytes 772
  32.6 77.6 %copy-start.7 = (f32[3072]{0:T(1024)S(1)}, f32[3072]{0:T(1024)}, u32[]{:S(2)}) copy-start(f32[3072]{0:T(1024)} %param.17) | copy-start | bytes 36868
  32.6 23.6 %copy-start.1 = (f32[4,16,32,128]{3,2,1,0:T(8,128)S(1)}, f32[4,16,32,128]{3,2,1,0:T(8,128)}, u32[]{:S(2)}) copy-start(f32[4,16,32,128]{3,2,1,0:T(8,128)} %copy-done) | copy-start | bytes 3145732
  32.6 23.6 %collective-permute-start.6 = (bf16[4,16,32,128]{3,2,1,0:T(8,128)(2,1)S(1)}, bf16[4,16,32,128]{3,2,1,0:T(8,128)(2,1)S(1)}, u32[]{:S(2)}, u32[]{:S(2)}) collective-permute-start(bf16[4,16,32,128]{3,2,1,0:T(8,128)(2,1)S(1)} %get-tuple-element.56), channel_id=1, source_target_pairs={{0,4},{4,0},{8,12},{12,8},{16,20},{20,16},{24,28},{28,24},{1,5},{5... | collective-permute-start | bytes 1572872 | tf_op jit(solution)/shard_map/ppermute | solution.py:336
  34.4 9.2 %collective-permute-start.8 = (bf16[43,24,128]{2,1,0:T(8,128)(2,1)S(1)}, bf16[43,24,128]{2,1,0:T(8,128)(2,1)S(1)}, u32[]{:S(2)}, u32[]{:S(2)}) collective-permute-start(bf16[43,24,128]{2,1,0:T(8,128)(2,1)S(1)} %copy-done.13), channel_id=1, source_target_pairs={{0,2},{1,3},{2,0},{3,1},{4,6},{5,7},{6,4},{7,5},{8,10},{9,11},{10,... | collective-permute-start | bytes 792584 | tf_op jit(solution)/shard_map/ppermute | solution.py:333
  35.9 12.4 %collective-permute-start.9 = (bf16[43,24,128]{2,1,0:T(8,128)(2,1)S(1)}, bf16[43,24,128]{2,1,0:T(8,128)(2,1)S(1)}, u32[]{:S(2)}, u32[]{:S(2)}) collective-permute-start(bf16[43,24,128]{2,1,0:T(8,128)(2,1)S(1)} %copy-done.12), channel_id=1, source_target_pairs={{0,3},{1,2},{2,1},{3,0},{4,7},{5,6},{6,5},{7,4},{8,11},{9,10},{10,... | collective-permute-start | bytes 792584 | tf_op jit(solution)/shard_map/ppermute | solution.py:333
  36.0 16.9 %collective-permute-start.14 = (bf16[43,24,128]{2,1,0:T(8,128)(2,1)}, bf16[43,24,128]{2,1,0:T(8,128)(2,1)S(1)}, u32[]{:S(2)}, u32[]{:S(2)}) collective-permute-start(bf16[43,24,128]{2,1,0:T(8,128)(2,1)} %get-tuple-element.67), channel_id=1, source_target_pairs={{0,1},{1,0},{2,3},{3,2},{4,5},{5,4},{6,7},{7,6},{8,9},{9,8},{10,11... | collective-permute-start | bytes 792584 | tf_op jit(solution)/shard_map/ppermute | solution.py:333
  36.5 17.7 %collective-permute-start.15 = (bf16[43,24,128]{2,1,0:T(8,128)(2,1)}, bf16[43,24,128]{2,1,0:T(8,128)(2,1)S(1)}, u32[]{:S(2)}, u32[]{:S(2)}) collective-permute-start(bf16[43,24,128]{2,1,0:T(8,128)(2,1)} %get-tuple-element.68), channel_id=1, source_target_pairs={{0,2},{1,3},{2,0},{3,1},{4,6},{5,7},{6,4},{7,5},{8,10},{9,11},{10,... | collective-permute-start | bytes 792584 | tf_op jit(solution)/shard_map/ppermute | solution.py:333
  48.3 0.9 copy-start.6
  50.6 11.9 %collective-permute-start.13 = (bf16[4,16,24,128]{3,2,1,0:T(8,128)(2,1)S(1)}, bf16[4,16,24,128]{3,2,1,0:T(8,128)(2,1)S(1)}, u32[]{:S(2)}, u32[]{:S(2)}) collective-permute-start(bf16[4,16,24,128]{3,2,1,0:T(8,128)(2,1)S(1)} %get-tuple-element.66), channel_id=1, source_target_pairs={{0,4},{4,0},{8,12},{12,8},{16,20},{20,16},{24,28},{28,24},{1,5},{5... | collective-permute-start | bytes 1179656 | tf_op jit(solution)/shard_map/ppermute | solution.py:336
  51.2 8.4 %collective-permute-start.16 = (bf16[43,24,128]{2,1,0:T(8,128)(2,1)S(1)}, bf16[43,24,128]{2,1,0:T(8,128)(2,1)S(1)}, u32[]{:S(2)}, u32[]{:S(2)}) collective-permute-start(bf16[43,24,128]{2,1,0:T(8,128)(2,1)S(1)} %copy-done.11), channel_id=1, source_target_pairs={{0,3},{1,2},{2,1},{3,0},{4,7},{5,6},{6,5},{7,4},{8,11},{9,10},{10,... | collective-permute-start | bytes 792584 | tf_op jit(solution)/shard_map/ppermute | solution.py:333
  52.8 9.8 %collective-permute-start.21 = (bf16[43,16,128]{2,1,0:T(8,128)(2,1)}, bf16[43,16,128]{2,1,0:T(8,128)(2,1)S(1)}, u32[]{:S(2)}, u32[]{:S(2)}) collective-permute-start(bf16[43,16,128]{2,1,0:T(8,128)(2,1)} %get-tuple-element.76), channel_id=1, source_target_pairs={{0,1},{1,0},{2,3},{3,2},{4,5},{5,4},{6,7},{7,6},{8,9},{9,8},{10,11... | collective-permute-start | bytes 528392 | tf_op jit(solution)/shard_map/ppermute | solution.py:333
  54.2 9.9 %collective-permute-start.22 = (bf16[43,16,128]{2,1,0:T(8,128)(2,1)}, bf16[43,16,128]{2,1,0:T(8,128)(2,1)S(1)}, u32[]{:S(2)}, u32[]{:S(2)}) collective-permute-start(bf16[43,16,128]{2,1,0:T(8,128)(2,1)} %get-tuple-element.77), channel_id=1, source_target_pairs={{0,2},{1,3},{2,0},{3,1},{4,6},{5,7},{6,4},{7,5},{8,10},{9,11},{10,... | collective-permute-start | bytes 528392 | tf_op jit(solution)/shard_map/ppermute | solution.py:333
  56.2 10.6 %collective-permute-start.23 = (bf16[43,16,128]{2,1,0:T(8,128)(2,1)}, bf16[43,16,128]{2,1,0:T(8,128)(2,1)S(1)}, u32[]{:S(2)}, u32[]{:S(2)}) collective-permute-start(bf16[43,16,128]{2,1,0:T(8,128)(2,1)} %get-tuple-element.78), channel_id=1, source_target_pairs={{0,3},{1,2},{2,1},{3,0},{4,7},{5,6},{6,5},{7,4},{8,11},{9,10},{10,... | collective-permute-start | bytes 528392 | tf_op jit(solution)/shard_map/ppermute | solution.py:333
  61.0 21.2 %collective-permute-start.20 = (bf16[4,16,24,128]{3,2,1,0:T(8,128)(2,1)S(1)}, bf16[4,16,24,128]{3,2,1,0:T(8,128)(2,1)S(1)}, u32[]{:S(2)}, u32[]{:S(2)}) collective-permute-start(bf16[4,16,24,128]{3,2,1,0:T(8,128)(2,1)S(1)} %get-tuple-element.75), channel_id=1, source_target_pairs={{0,4},{4,0},{8,12},{12,8},{16,20},{20,16},{24,28},{28,24},{1,5},{5... | collective-permute-start | bytes 1179656 | tf_op jit(solution)/shard_map/ppermute | solution.py:336
  68.3 10.2 %collective-permute-start.27 = (bf16[4,16,16,128]{3,2,1,0:T(8,128)(2,1)S(1)}, bf16[4,16,16,128]{3,2,1,0:T(8,128)(2,1)S(1)}, u32[]{:S(2)}, u32[]{:S(2)}) collective-permute-start(bf16[4,16,16,128]{3,2,1,0:T(8,128)(2,1)S(1)} %get-tuple-element.84), channel_id=1, source_target_pairs={{0,4},{4,0},{8,12},{12,8},{16,20},{20,16},{24,28},{28,24},{1,5},{5... | collective-permute-start | bytes 786440 | tf_op jit(solution)/shard_map/ppermute | solution.py:336
  69.8 5.2 %collective-permute-start.17 = (bf16[1,16,24,128]{3,2,1,0:T(8,128)(2,1)S(1)}, bf16[1,16,24,128]{3,2,1,0:T(8,128)(2,1)S(1)}, u32[]{:S(2)}, u32[]{:S(2)}) collective-permute-start(bf16[1,16,24,128]{3,2,1,0:T(8,128)(2,1)S(1)} %get-tuple-element.72), channel_id=1, source_target_pairs={{0,8},{4,12},{8,0},{12,4},{16,24},{20,28},{24,16},{28,20},{1,9},{5... | collective-permute-start | bytes 294920 | tf_op jit(solution)/shard_map/ppermute | solution.py:336
  71.3 11.2 %collective-permute-start.18 = (bf16[1,16,24,128]{3,2,1,0:T(8,128)(2,1)S(1)}, bf16[1,16,24,128]{3,2,1,0:T(8,128)(2,1)S(1)}, u32[]{:S(2)}, u32[]{:S(2)}) collective-permute-start(bf16[1,16,24,128]{3,2,1,0:T(8,128)(2,1)S(1)} %get-tuple-element.73), channel_id=1, source_target_pairs={{0,16},{4,20},{8,24},{12,28},{16,0},{20,4},{24,8},{28,12},{1,17},{... | collective-permute-start | bytes 294920 | tf_op jit(solution)/shard_map/ppermute | solution.py:336
  73.9 23.5 %collective-permute-start.10 = (bf16[1,16,32,128]{3,2,1,0:T(8,128)(2,1)S(1)}, bf16[1,16,32,128]{3,2,1,0:T(8,128)(2,1)S(1)}, u32[]{:S(2)}, u32[]{:S(2)}) collective-permute-start(bf16[1,16,32,128]{3,2,1,0:T(8,128)(2,1)S(1)} %get-tuple-element.63), channel_id=1, source_target_pairs={{0,8},{4,12},{8,0},{12,4},{16,24},{20,28},{24,16},{28,20},{1,9},{5... | collective-permute-start | bytes 393224 | tf_op jit(solution)/shard_map/ppermute | solution.py:336
  75.0 22.9 %collective-permute-start.11 = (bf16[1,16,32,128]{3,2,1,0:T(8,128)(2,1)S(1)}, bf16[1,16,32,128]{3,2,1,0:T(8,128)(2,1)S(1)}, u32[]{:S(2)}, u32[]{:S(2)}) collective-permute-start(bf16[1,16,32,128]{3,2,1,0:T(8,128)(2,1)S(1)} %get-tuple-element.64), channel_id=1, source_target_pairs={{0,16},{4,20},{8,24},{12,28},{16,0},{20,4},{24,8},{28,12},{1,17},{... | collective-permute-start | bytes 393224 | tf_op jit(solution)/shard_map/ppermute | solution.py:336
  78.6 19.4 %collective-permute-start.12 = (bf16[1,16,32,128]{3,2,1,0:T(8,128)(2,1)S(1)}, bf16[1,16,32,128]{3,2,1,0:T(8,128)(2,1)S(1)}, u32[]{:S(2)}, u32[]{:S(2)}) collective-permute-start(bf16[1,16,32,128]{3,2,1,0:T(8,128)(2,1)S(1)} %get-tuple-element.65), channel_id=1, source_target_pairs={{0,24},{4,28},{8,16},{12,20},{16,8},{20,12},{24,0},{28,4},{1,25},{... | collective-permute-start | bytes 393224 | tf_op jit(solution)/shard_map/ppermute | solution.py:336
  82.1 8.1 %collective-permute-start.19 = (bf16[1,16,24,128]{3,2,1,0:T(8,128)(2,1)S(1)}, bf16[1,16,24,128]{3,2,1,0:T(8,128)(2,1)S(1)}, u32[]{:S(2)}, u32[]{:S(2)}) collective-permute-start(bf16[1,16,24,128]{3,2,1,0:T(8,128)(2,1)S(1)} %get-tuple-element.74), channel_id=1, source_target_pairs={{0,24},{4,28},{8,16},{12,20},{16,8},{20,12},{24,0},{28,4},{1,25},{... | collective-permute-start | bytes 294920 | tf_op jit(solution)/shard_map/ppermute | solution.py:336
  82.6 19.2 %collective-permute-start.28 = (bf16[1,16,16,128]{3,2,1,0:T(8,128)(2,1)S(1)}, bf16[1,16,16,128]{3,2,1,0:T(8,128)(2,1)S(1)}, u32[]{:S(2)}, u32[]{:S(2)}) collective-permute-start(bf16[1,16,16,128]{3,2,1,0:T(8,128)(2,1)S(1)} %get-tuple-element.86), channel_id=1, source_target_pairs={{0,8},{4,12},{8,0},{12,4},{16,24},{20,28},{24,16},{28,20},{1,9},{5... | collective-permute-start | bytes 196616 | tf_op jit(solution)/shard_map/ppermute | solution.py:336
  90.2 12.3 %collective-permute-start.29 = (bf16[1,16,16,128]{3,2,1,0:T(8,128)(2,1)S(1)}, bf16[1,16,16,128]{3,2,1,0:T(8,128)(2,1)S(1)}, u32[]{:S(2)}, u32[]{:S(2)}) collective-permute-start(bf16[1,16,16,128]{3,2,1,0:T(8,128)(2,1)S(1)} %get-tuple-element.87), channel_id=1, source_target_pairs={{0,16},{4,20},{8,24},{12,28},{16,0},{20,4},{24,8},{28,12},{1,17},{... | collective-permute-start | bytes 196616 | tf_op jit(solution)/shard_map/ppermute | solution.py:336
  97.4 6.9 %collective-permute-start.30 = (bf16[1,16,16,128]{3,2,1,0:T(8,128)(2,1)S(1)}, bf16[1,16,16,128]{3,2,1,0:T(8,128)(2,1)S(1)}, u32[]{:S(2)}, u32[]{:S(2)}) collective-permute-start(bf16[1,16,16,128]{3,2,1,0:T(8,128)(2,1)S(1)} %get-tuple-element.88), channel_id=1, source_target_pairs={{0,24},{4,28},{8,16},{12,20},{16,8},{20,12},{24,0},{28,4},{1,25},{... | collective-permute-start | bytes 196616 | tf_op jit(solution)/shard_map/ppermute | solution.py:336
  97.8 6.4 %collective-permute-start.24 = (bf16[1,16,24,128]{3,2,1,0:T(8,128)(2,1)S(1)}, bf16[1,16,24,128]{3,2,1,0:T(8,128)(2,1)S(1)}, u32[]{:S(2)}, u32[]{:S(2)}) collective-permute-start(bf16[1,16,24,128]{3,2,1,0:T(8,128)(2,1)S(1)} %get-tuple-element.81), channel_id=1, source_target_pairs={{0,8},{4,12},{8,0},{12,4},{16,24},{20,28},{24,16},{28,20},{1,9},{5... | collective-permute-start | bytes 294920 | tf_op jit(solution)/shard_map/ppermute | solution.py:336
  98.0 12.3 %collective-permute-start.25 = (bf16[1,16,24,128]{3,2,1,0:T(8,128)(2,1)S(1)}, bf16[1,16,24,128]{3,2,1,0:T(8,128)(2,1)S(1)}, u32[]{:S(2)}, u32[]{:S(2)}) collective-permute-start(bf16[1,16,24,128]{3,2,1,0:T(8,128)(2,1)S(1)} %get-tuple-element.82), channel_id=1, source_target_pairs={{0,16},{4,20},{8,24},{12,28},{16,0},{20,4},{24,8},{28,12},{1,17},{... | collective-permute-start | bytes 294920 | tf_op jit(solution)/shard_map/ppermute | solution.py:336
  101.8 8.5 %collective-permute-start.26 = (bf16[1,16,24,128]{3,2,1,0:T(8,128)(2,1)S(1)}, bf16[1,16,24,128]{3,2,1,0:T(8,128)(2,1)S(1)}, u32[]{:S(2)}, u32[]{:S(2)}) collective-permute-start(bf16[1,16,24,128]{3,2,1,0:T(8,128)(2,1)S(1)} %get-tuple-element.83), channel_id=1, source_target_pairs={{0,24},{4,28},{8,16},{12,20},{16,8},{20,12},{24,0},{28,4},{1,25},{... | collective-permute-start | bytes 294920 | tf_op jit(solution)/shard_map/ppermute | solution.py:336
where the time goes:
time: 112 us
  starting transfers between devices  42 us (38%)
  waiting for transfers between devices  41.8 us (37%)
  Pallas kernels  24.4 us (22%)
  local copies, waits for them, and re-layouts  3.14 us (3%)
    ppermute x16, starting transfers between devices, swap_blk(): return lax.ppermute(value, 'blk', [(i, i ^ k) for i in range(blk_count)])  29.3 us
    ppermute x15, waiting for transfers between devices, swap_rep(): return lax.ppermute(value, 'rep', [(i, i ^ k) for i in range(rep_count)])  25.8 us
    pallas_call x4, Pallas kernels, partials(): pl.pallas_call(functools.partial(partial_kernel, span, owned, len(tables)...  16.8 us
    ppermute x16, waiting for transfers between devices, swap_blk(): return lax.ppermute(value, 'blk', [(i, i ^ k) for i in range(blk_count)])  16 us
    ppermute x15, starting transfers between devices, swap_rep(): return lax.ppermute(value, 'rep', [(i, i ^ k) for i in range(rep_count)])  12.7 us
    pallas_call x4, Pallas kernels, gather_tiles(): pl.pallas_call(functools.partial(gather_kernel, len(ids), factor), out_sh...  5.83 us
    unnamed x28, local copies, waits for them, and re-layouts  2.88 us
  transfers between devices with their start and end apart: 31, of which 12 were waited for; matrix products, arithmetic and copies ran while one was open for 0% of the time, Pallas kernels for 16%

commit v1 on v0

--- a/solution.py
+++ b/solution.py
@@ -8,8 +8,9 @@
 from jax.sharding import PartitionSpec as P
 
 LANES = 128
-COPY_PANELS = 11
+COPY_PANELS = 43
 SHARES = (4, 3, 3, 2)
+MAKES = ((1, -3), (1, -2), (1, -1), (1, 0.4))
 
 
 def stage_factors(count):
@@ -22,9 +23,16 @@
 
 
 def task_order(parts, stages):
-    keys = [(part - 2.6, part, -1) for part in range(parts)]
-    keys += [(part + 1.5 * stage, part, stage) for part in range(parts) for stage in range(stages)]
-    return [(part, stage) for _, part, stage in sorted(keys)]
+    keys, start = [], 0
+    for size, when in MAKES:
+        keys.append((when, range(start, min(start + size, parts)), -1))
+        start += size
+    keys += [
+        (part + 1.5 * stage, range(part, part + 1), stage)
+        for part in range(parts)
+        for stage in range(stages)
+    ]
+    return [(group, stage) for _, group, stage in sorted(keys, key=lambda item: item[0])]
 
 
 def whole(memory_space=pltpu.VMEM):
@@ -81,10 +89,11 @@
     return target_row, keep.astype(jnp.float32)
 
 
-def partial_kernel(span, owned, tables, extra, *refs):
+def partial_kernel(spans, owned, tables, *refs):
     amp, panels = refs[tables : tables + 2]
-    outs = refs[tables + 2 + extra :]
-    copied, (buffer, amp_here, sem, small) = outs[-4 - tables : -4], outs[-4:]
+    outs, (amp_here, sem, small) = refs[tables + 2 : -3], refs[-3:]
+    buffers = outs[-len(spans) :]
+    copied = outs[-len(spans) - tables : -len(spans)]
     rep_count, row_count, depth = amp.shape
     count = panels.shape[0]
     loads = [
@@ -93,16 +102,18 @@
     ]
     for load in loads:
         load.start()
-    first, rows = span
     copies = []
-    for start in range(0, count, COPY_PANELS):
-        piece = pl.ds(start, min(COPY_PANELS, count - start))
-        copies.append(
-            pltpu.make_async_copy(
-                panels.at[piece, :, pl.ds(first, rows)], buffer.at[piece], sem.at[len(copies)]
+    for (first, rows), buffer in zip(spans, buffers):
+        for start in range(0, count, COPY_PANELS):
+            piece = pl.ds(start, min(COPY_PANELS, count - start))
+            copies.append(
+                pltpu.make_async_copy(
+                    panels.at[piece, :, pl.ds(first, rows)],
+                    buffer.at[piece],
+                    sem.at[len(copies)],
+                )
             )
-        )
-        copies[-1].start()
+            copies[-1].start()
     for load in loads:
         load.wait()
 
@@ -115,28 +126,30 @@
     else:
         factors = copied[0]
 
-    for copy in copies:
-        copy.wait()
-    halves = buffer.shape[1]
     factor = factors[...].astype(jnp.bfloat16)
-    live_panels = buffer[...] * factor[:, None, None, :]
-    product = jnp.dot(
-        live_panels.reshape(count * halves * rows, depth),
-        amp_t,
-        preferred_element_type=jnp.float32,
-    )
-    product = product.reshape(count, halves, rows, rep_count * row_count)
-    for pair in range(rep_count // 2):
-        lanes = slice(pair * LANES, (pair + 1) * LANES)
-        packed = half_rows(product[:, 0, :, lanes], product[:, 1, :, lanes])
-        for side, value in enumerate(packed):
-            outs[2 * pair + side][...] = value.astype(jnp.bfloat16)
-
-
-def partials(tables, amp, panels, span, owned, after=None):
+    pieces = len(copies) // len(spans)
+    for part, ((_, rows), buffer) in enumerate(zip(spans, buffers)):
+        for copy in copies[part * pieces : (part + 1) * pieces]:
+            copy.wait()
+        halves = buffer.shape[1]
+        live_panels = buffer[...] * factor[:, None, None, :]
+        product = jnp.dot(
+            live_panels.reshape(count * halves * rows, depth),
+            amp_t,
+            preferred_element_type=jnp.float32,
+        )
+        product = product.reshape(count, halves, rows, rep_count * row_count)
+        for pair in range(rep_count // 2):
+            lanes = slice(pair * LANES, (pair + 1) * LANES)
+            packed = half_rows(product[:, 0, :, lanes], product[:, 1, :, lanes])
+            for side, value in enumerate(packed):
+                outs[part * rep_count + 2 * pair + side][...] = value.astype(jnp.bfloat16)
+
+
+def partials(tables, amp, panels, spans, owned):
     count, halves, _, depth = panels.shape
     rep_count, row_count, _ = amp.shape
-    rows = span[1]
+    total = sum(rows for _, rows in spans)
     outs = []
     if len(tables) > 1:
         outs += [
@@ -144,31 +157,34 @@
             jax.ShapeDtypeStruct((count, depth), jnp.float32),
         ]
     heads = len(outs)
-    outs += [jax.ShapeDtypeStruct((count, rows, LANES), jnp.bfloat16)] * rep_count
-    extra = [] if after is None else [after]
+    for _, rows in spans:
+        outs += [jax.ShapeDtypeStruct((count, rows, LANES), jnp.bfloat16)] * rep_count
     results = pl.pallas_call(
-        functools.partial(partial_kernel, span, owned, len(tables), len(extra)),
+        functools.partial(partial_kernel, spans, owned, len(tables)),
         out_shape=outs,
-        in_specs=[whole(pl.ANY)] * (len(tables) + 2 + len(extra)),
+        in_specs=[whole(pl.ANY)] * (len(tables) + 2),
         out_specs=[whole()] * len(outs),
         scratch_shapes=[
             *[pltpu.VMEM(t.shape, t.dtype) for t in tables],
-            pltpu.VMEM((count, halves, rows, depth), jnp.bfloat16),
+            *[pltpu.VMEM((count, halves, rows, depth), jnp.bfloat16) for _, rows in spans],
             pltpu.VMEM(amp.shape, amp.dtype),
-            pltpu.SemaphoreType.DMA((pl.cdiv(count, COPY_PANELS),)),
+            pltpu.SemaphoreType.DMA((pl.cdiv(count, COPY_PANELS) * len(spans),)),
             pltpu.SemaphoreType.DMA((len(tables) + 1,)),
         ],
         compiler_params=pltpu.CompilerParams(
             vmem_limit_bytes=(62 << 20) if heads else (66 << 20) - nbytes(panels)
         ),
         cost_estimate=pl.CostEstimate(
-            flops=2 * count * halves * rows * depth * rep_count * row_count,
-            bytes_accessed=2 * count * halves * rows * (depth + rep_count * row_count),
+            flops=2 * count * halves * total * depth * rep_count * row_count,
+            bytes_accessed=2 * count * halves * total * (depth + rep_count * row_count),
             transcendentals=0,
         ),
         name="partials",
-    )(*tables, amp, panels, *extra)
-    return results[:heads], results[heads:]
+    )(*tables, amp, panels)
+    parts = results[heads:]
+    return results[:heads], [
+        parts[i * rep_count : (i + 1) * rep_count] for i in range(len(spans))
+    ]
 
 
 def gather_kernel(count_ids, factor, *refs):
@@ -201,19 +217,17 @@
             outs[k][z] = (ladders[0][span] + ladders[1][span]).astype(outs[k].dtype)
 
 
-def gather_tiles(ids, parts, blk_count, tiles, factor, after=None):
+def gather_tiles(ids, parts, blk_count, tiles, factor):
     _, rows, _ = parts[0].shape
     shape = (blk_count // factor, tiles, rows, LANES)
     outs = [jax.ShapeDtypeStruct(shape, jnp.bfloat16 if k else jnp.float32) for k in range(factor)]
     ladder = pltpu.VMEM((blk_count * tiles, rows, LANES), jnp.float32)
-    extra = [] if after is None else [after]
     return pl.pallas_call(
         functools.partial(gather_kernel, len(ids), factor),
         out_shape=outs,
         in_specs=[whole(pltpu.SMEM)] * len(ids)
         + [whole(pl.ANY)]
-        + [whole()] * (len(parts) - 1)
-        + [whole(pl.ANY)] * len(extra),
+        + [whole()] * (len(parts) - 1),
         out_specs=[whole()] * factor,
         scratch_shapes=[ladder] * 2
         + [pltpu.VMEM(parts[0].shape, parts[0].dtype), pltpu.SemaphoreType.DMA],
@@ -224,7 +238,7 @@
             transcendentals=0,
         ),
         name="gather_tiles",
-    )(*ids, *parts, *extra)
+    )(*ids, *parts)
 
 
 def merge_kernel(arrays, factor, stride, *refs):
@@ -240,15 +254,14 @@
             outs[k][z] = total.astype(outs[k].dtype)
 
 
-def merge(arrays, factor, stride, after=None):
+def merge(arrays, factor, stride):
     owners, tiles, rows, _ = arrays[0].shape
     shape = (owners // factor, tiles, rows, LANES)
     outs = [jax.ShapeDtypeStruct(shape, jnp.bfloat16 if k else jnp.float32) for k in range(factor)]
-    extra = [] if after is None else [after]
     return pl.pallas_call(
         functools.partial(merge_kernel, len(arrays), factor, stride),
         out_shape=outs,
-        in_specs=[whole()] * len(arrays) + [whole(pl.ANY)] * len(extra),
+        in_specs=[whole()] * len(arrays),
         out_specs=[whole()] * factor,
         compiler_params=grant(*arrays, *outs),
         cost_estimate=pl.CostEstimate(
@@ -257,7 +270,7 @@
             transcendentals=0,
         ),
         name="merge",
-    )(*arrays, *extra)
+    )(*arrays)
 
 
 def finish_kernel(per_part, *refs):
@@ -341,29 +354,30 @@
         spans.append((first, rows))
         first += rows
 
-    last, ids, strides = None, None, [1]
+    ids, strides = None, [1]
     for factor in factors:
         strides.append(strides[-1] * factor)
     pending = [None] * len(spans)
-    for part, stage in task_order(len(spans), len(factors)):
+    for group, stage in task_order(len(spans), len(factors)):
         if stage < 0:
-            heads, (own, *others) = partials(tables, amp, panels, spans[part], owned, last)
-            last = own
+            group_spans = [spans[part] for part in group]
+            heads, made = partials(tables, amp, panels, group_spans, owned)
         elif stage == 0:
-            arrays = gather_tiles(ids, pending[part], blk_count, owned, factors[0], last)
-            last = arrays[0]
+            part = group[0]
+            arrays = gather_tiles(ids, pending[part], blk_count, owned, factors[0])
         else:
-            arrays = merge(pending[part], factors[stage], strides[stage], last)
-            last = arrays[0]
+            part = group[0]
+            arrays = merge(pending[part], factors[stage], strides[stage])
         if stage < 0:
-            swapped = [swap_rep(others[k - 1], k) for k in range(1, rep_count)]
-            pending[part] = [own, *swapped]
+            for part, (own, *others) in zip(group, made):
+                swapped = [swap_rep(others[k - 1], k) for k in range(1, rep_count)]
+                pending[part] = [own, *swapped]
             if heads:
                 tables = heads[1:]
                 ids = [heads[0]] + [swap_rep(heads[0], k) for k in range(1, rep_count)]
         else:
-            stride = strides[stage]
-            swapped = [swap_blk(arrays[k], k * stride) for k in range(1, factors[stage])]
+            stride, peers = strides[stage], factors[stage]
+            swapped = [swap_blk(arrays[k], k * stride) for k in range(1, peers)]
             pending[part] = [arrays[0], *swapped]
     collected = [value[0] for part in pending for value in part]
 

time: 112 us -> 124 us (1.11)
  waiting for transfers between devices: 41.8 us -> 57.8 us
  starting transfers between devices: 42 us -> 38.6 us
  local copies, waits for them, and re-layouts: 3.14 us -> 1.22 us
  Pallas kernels: 24.4 us -> 26.3 us
    ppermute x16, waiting for transfers between devices: 16 us -> 34.9 us  [swap_blk(): return lax.ppermute(value, 'blk', [(i, i ^ k) for i in range(blk_count)])]
    ppermute x16, starting transfers between devices: 29.3 us -> 25.1 us  [swap_blk(): return lax.ppermute(value, 'blk', [(i, i ^ k) for i in range(blk_count)])]
    ppermute x15, waiting for transfers between devices: 25.8 us -> 22.9 us  [swap_rep(): return lax.ppermute(value, 'rep', [(i, i ^ k) for i in range(rep_count)])]
    unnamed x28 -> x22, local copies, waits for them, and re-layouts: 2.88 us -> 0.97 us
    pallas_call x4, Pallas kernels: 0.39 us -> 2.17 us  [merge(): pl.pallas_call(functools.partial(merge_kernel, len(arrays), factor, strid...]
  transfers between devices with their start and end apart: 31 -> 31, of which waited for: 12 -> 13; matrix products, arithmetic and copies ran while one was open for 0% -> 0% of each run, Pallas kernels for 16% -> 13%
where the time goes in v1:
time: 124 us
  waiting for transfers between devices  57.8 us (47%)
  starting transfers between devices  38.6 us (31%)
  Pallas kernels  26.3 us (21%)
    ppermute x16, waiting for transfers between devices, swap_blk(): return lax.ppermute(value, 'blk', [(i, i ^ k) for i in range(blk_count)])  34.9 us
    ppermute x16, starting transfers between devices, swap_blk(): return lax.ppermute(value, 'blk', [(i, i ^ k) for i in range(blk_count)])  25.1 us
    ppermute x15, waiting for transfers between devices, swap_rep(): return lax.ppermute(value, 'rep', [(i, i ^ k) for i in range(rep_count)])  22.9 us
    pallas_call x4, Pallas kernels, partials(): pl.pallas_call(functools.partial(partial_kernel, spans, owned, len(tables...  16.9 us
    ppermute x15, starting transfers between devices, swap_rep(): return lax.ppermute(value, 'rep', [(i, i ^ k) for i in range(rep_count)])  13.5 us
    pallas_call x4, Pallas kernels, gather_tiles(): pl.pallas_call(functools.partial(gather_kernel, len(ids), factor), out_sh...  5.83 us
  transfers between devices with their start and end apart: 31, of which 13 were waited for; matrix products, arithmetic and copies ran while one was open for 0% of the time, Pallas kernels for 13%

profile of v1, /device:TPU:0, one launch (start us, length us, event | category | flops | bytes accessed | tf_op | source)
XLA Modules:
  0.0 124.3 jit_solution(15441609124409164161)
XLA Ops:
  0.0 4.9 %partials.4 = (s32[1,43]{1,0:T(1,128)}, f32[43,768]{1,0:T(8,128)}, bf16[43,32,128]{2,1,0:T(8,128)(2,1)}, bf16[43,32,128]{2,1,0:T(8,128)(2,1)}, bf16[43,32,128]{2...) custom-call(s32[1,43]{1,0:T(1,128)} %bitcast.48, s32[43]{0:T(128)} %refs_1_.1, s32[4,43]{1,0:T(4,128)} %bitcast.47, s32[128]{0:T(128)} %refs_3_.1, ...), custom_call_target="tpu_custom_call" | custom-call | flops 1082130432 | bytes 5636096 | tf_op jit(solution)/shard_map/partials/pallas_call | solution.py:162
  5.0 4.3 %partials.5 = (bf16[43,24,128]{2,1,0:T(8,128)(2,1)}, bf16[43,24,128]{2,1,0:T(8,128)(2,1)}, bf16[43,24,128]{2,1,0:T(8,128)(2,1)}, bf16[43,24,128]{2,1,0:T(8,128)(2,1)}) custom-call(f32[43,768]{1,0:T(8,128)} %get-tuple-element.58.refs_0_, bf16[4,64,768]{2,1,0:T(8,128)(2,1)} %bitcast.44, bf16[43,2,96,768]{3,2,1,0:T(8,128)(2,1)} %bitcast.40), custom_call_target="tpu_custom_call" | custom-call | flops 811597824 | bytes 4227072 | tf_op jit(solution)/shard_map/partials/pallas_call | solution.py:162
  9.3 0.6 collective-permute-start.10
  9.8 2.6 %collective-permute-start.11 = (bf16[43,24,128]{2,1,0:T(8,128)(2,1)}, bf16[43,24,128]{2,1,0:T(8,128)(2,1)S(1)}, u32[]{:S(2)}, u32[]{:S(2)}) collective-permute-start(bf16[43,24,128]{2,1,0:T(8,128)(2,1)} %get-tuple-element.61), channel_id=1, source_target_pairs={{0,2},{1,3},{2,0},{3,1},{4,6},{5,7},{6,4},{7,5},{8,10},{9,11},{10,... | collective-permute-start | bytes 792584 | tf_op jit(solution)/shard_map/ppermute | solution.py:346
  12.4 0.0 collective-permute-start.12
  12.4 0.2 collective-permute-start
  12.6 1.9 %collective-permute-start.1 = (s32[1,43]{1,0:T(1,128)S(1)}, s32[1,43]{1,0:T(1,128)S(1)}, u32[]{:S(2)}, u32[]{:S(2)}) collective-permute-start(s32[1,43]{1,0:T(1,128)S(1)} %copy-done.5), channel_id=1, source_target_pairs={{0,2},{1,3},{2,0},{3,1},{4,6},{5,7},{6,4},{7,5},{8,10},{9,11},{10,... | collective-permute-start | bytes 524 | tf_op jit(solution)/shard_map/ppermute | solution.py:346
  14.5 4.2 %partials.6 = (bf16[43,24,128]{2,1,0:T(8,128)(2,1)}, bf16[43,24,128]{2,1,0:T(8,128)(2,1)}, bf16[43,24,128]{2,1,0:T(8,128)(2,1)}, bf16[43,24,128]{2,1,0:T(8,128)(2,1)}) custom-call(f32[43,768]{1,0:T(8,128)} %get-tuple-element.58.refs_0_, bf16[4,64,768]{2,1,0:T(8,128)(2,1)} %bitcast.45, bf16[43,2,96,768]{3,2,1,0:T(8,128)(2,1)} %bitcast.41), custom_call_target="tpu_custom_call" | custom-call | flops 811597824 | bytes 4227072 | tf_op jit(solution)/shard_map/partials/pallas_call | solution.py:162
  18.8 0.0 copy-start.6
  18.8 0.0 copy-start.7
  18.8 0.0 copy-start.4
  18.8 0.0 collective-permute-done.refs_1_
  18.8 0.1 collective-permute-start.2
  18.9 6.3 %collective-permute-done.1.refs_2_ = s32[1,43]{1,0:T(1,128)S(1)} collective-permute-done((s32[1,43]{1,0:T(1,128)S(1)}, s32[1,43]{1,0:T(1,128)S(1)}, u32[]{:S(2)}, u32[]{:S(2)}) %collective-permute-start.1) | collective-permute-done | bytes 204 | tf_op jit(solution)/shard_map/ppermute | solution.py:346
  25.2 0.0 collective-permute-start.17
  25.2 0.0 collective-permute-done.2.refs_3_
  25.2 0.5 collective-permute-start.3
  25.8 1.7 %collective-permute-start.4 = (bf16[43,32,128]{2,1,0:T(8,128)(2,1)S(1)}, bf16[43,32,128]{2,1,0:T(8,128)(2,1)S(1)}, u32[]{:S(2)}, u32[]{:S(2)}) collective-permute-start(bf16[43,32,128]{2,1,0:T(8,128)(2,1)S(1)} %copy-done.9), channel_id=1, source_target_pairs={{0,2},{1,3},{2,0},{3,1},{4,6},{5,7},{6,4},{7,5},{8,10},{9,11},{10,... | collective-permute-start | bytes 1056776 | tf_op jit(solution)/shard_map/ppermute | solution.py:346
  27.5 1.4 %collective-permute-start.18 = (bf16[43,24,128]{2,1,0:T(8,128)(2,1)}, bf16[43,24,128]{2,1,0:T(8,128)(2,1)S(1)}, u32[]{:S(2)}, u32[]{:S(2)}) collective-permute-start(bf16[43,24,128]{2,1,0:T(8,128)(2,1)} %get-tuple-element.71), channel_id=1, source_target_pairs={{0,2},{1,3},{2,0},{3,1},{4,6},{5,7},{6,4},{7,5},{8,10},{9,11},{10,... | collective-permute-start | bytes 792584 | tf_op jit(solution)/shard_map/ppermute | solution.py:346
  28.9 0.4 collective-permute-start.19
  29.3 3.5 %partials.7 = (bf16[43,16,128]{2,1,0:T(8,128)(2,1)}, bf16[43,16,128]{2,1,0:T(8,128)(2,1)}, bf16[43,16,128]{2,1,0:T(8,128)(2,1)}, bf16[43,16,128]{2,1,0:T(8,128)(2,1)}) custom-call(f32[43,768]{1,0:T(8,128)} %get-tuple-element.58.refs_0_, bf16[4,64,768]{2,1,0:T(8,128)(2,1)} %bitcast.46, bf16[43,2,96,768]{3,2,1,0:T(8,128)(2,1)} %bitcast.42), custom_call_target="tpu_custom_call" | custom-call | flops 541065216 | bytes 2818048 | tf_op jit(solution)/shard_map/partials/pallas_call | solution.py:162
  32.8 0.5 collective-permute-start.24
  33.3 3.5 %collective-permute-done.4.refs_6_ = bf16[43,32,128]{2,1,0:T(8,128)(2,1)S(1)} collective-permute-done((bf16[43,32,128]{2,1,0:T(8,128)(2,1)S(1)}, bf16[43,32,128]{2,1,0:T(8,128)(2,1)S(1)}, u32[]{:S(2)}, u32[]{:S(2)}) %collective-permute-start.4) | collective-permute-done | bytes 352288 | tf_op jit(solution)/shard_map/ppermute | solution.py:346
  36.9 1.7 %collective-permute-start.25 = (bf16[43,16,128]{2,1,0:T(8,128)(2,1)}, bf16[43,16,128]{2,1,0:T(8,128)(2,1)S(1)}, u32[]{:S(2)}, u32[]{:S(2)}) collective-permute-start(bf16[43,16,128]{2,1,0:T(8,128)(2,1)} %get-tuple-element.81), channel_id=1, source_target_pairs={{0,2},{1,3},{2,0},{3,1},{4,6},{5,7},{6,4},{7,5},{8,10},{9,11},{10,... | collective-permute-start | bytes 528392 | tf_op jit(solution)/shard_map/ppermute | solution.py:346
  38.6 5.1 %collective-permute-done.5.refs_7_ = bf16[43,32,128]{2,1,0:T(8,128)(2,1)S(1)} collective-permute-done((bf16[43,32,128]{2,1,0:T(8,128)(2,1)S(1)}, bf16[43,32,128]{2,1,0:T(8,128)(2,1)S(1)}, u32[]{:S(2)}, u32[]{:S(2)}) %collective-permute-start.5) | collective-permute-done | bytes 352288 | tf_op jit(solution)/shard_map/ppermute | solution.py:346
  43.7 1.9 %collective-permute-start.26 = (bf16[43,16,128]{2,1,0:T(8,128)(2,1)}, bf16[43,16,128]{2,1,0:T(8,128)(2,1)S(1)}, u32[]{:S(2)}, u32[]{:S(2)}) collective-permute-start(bf16[43,16,128]{2,1,0:T(8,128)(2,1)} %get-tuple-element.82), channel_id=1, source_target_pairs={{0,3},{1,2},{2,1},{3,0},{4,7},{5,6},{6,5},{7,4},{8,11},{9,10},{10,... | collective-permute-start | bytes 528392 | tf_op jit(solution)/shard_map/ppermute | solution.py:346
  45.6 1.7 %gather_tiles.4 = (f32[4,16,32,128]{3,2,1,0:T(8,128)S(1)}, bf16[4,16,32,128]{3,2,1,0:T(8,128)(2,1)S(1)}) custom-call(s32[1,43]{1,0:T(1,128)S(1)} %copy-done.5, s32[1,43]{1,0:T(1,128)S(1)} %collective-permute-done.refs_1_, s32[1,43]{1,0:T(1,128)S(1)} %collective-permute-done.1.refs_2_, s32[1,43]{1,0:T(1,128)S(1)} %collective-permute-done.2.refs_3_, ...), custom_call_target="tpu_custom_call" | custom-call | flops 524288 | bytes 4194304 | tf_op jit(solution)/shard_map/gather_tiles/pallas_call | solution.py:225
  47.3 2.8 %collective-permute-done.18.refs_6_ = bf16[43,24,128]{2,1,0:T(8,128)(2,1)S(1)} collective-permute-done((bf16[43,24,128]{2,1,0:T(8,128)(2,1)}, bf16[43,24,128]{2,1,0:T(8,128)(2,1)S(1)}, u32[]{:S(2)}, u32[]{:S(2)}) %collective-permute-start.18) | collective-permute-done | bytes 264224 | tf_op jit(solution)/shard_map/ppermute | solution.py:346
  50.1 1.7 %collective-permute-start.6 = (bf16[4,16,32,128]{3,2,1,0:T(8,128)(2,1)S(1)}, bf16[4,16,32,128]{3,2,1,0:T(8,128)(2,1)S(1)}, u32[]{:S(2)}, u32[]{:S(2)}) collective-permute-start(bf16[4,16,32,128]{3,2,1,0:T(8,128)(2,1)S(1)} %get-tuple-element.53), channel_id=1, source_target_pairs={{0,4},{4,0},{8,12},{12,8},{16,20},{20,16},{24,28},{28,24},{1,5},{5... | collective-permute-start | bytes 1572872 | tf_op jit(solution)/shard_map/ppermute | solution.py:349
  51.8 1.4 %gather_tiles.5 = (f32[4,16,24,128]{3,2,1,0:T(8,128)S(1)}, bf16[4,16,24,128]{3,2,1,0:T(8,128)(2,1)S(1)}) custom-call(s32[1,43]{1,0:T(1,128)S(1)} %copy-done.5, s32[1,43]{1,0:T(1,128)S(1)} %collective-permute-done.refs_1_, s32[1,43]{1,0:T(1,128)S(1)} %collective-permute-done.1.refs_2_, s32[1,43]{1,0:T(1,128)S(1)} %collective-permute-done.2.refs_3_, ...), custom_call_target="tpu_custom_call" | custom-call | flops 393216 | bytes 3145728 | tf_op jit(solution)/shard_map/gather_tiles/pallas_call | solution.py:225
  53.2 1.9 %collective-permute-done.19.refs_7_ = bf16[43,24,128]{2,1,0:T(8,128)(2,1)S(1)} collective-permute-done((bf16[43,24,128]{2,1,0:T(8,128)(2,1)}, bf16[43,24,128]{2,1,0:T(8,128)(2,1)S(1)}, u32[]{:S(2)}, u32[]{:S(2)}) %collective-permute-start.19) | collective-permute-done | bytes 264224 | tf_op jit(solution)/shard_map/ppermute | solution.py:346
  55.1 1.5 %collective-permute-start.13 = (bf16[4,16,24,128]{3,2,1,0:T(8,128)(2,1)S(1)}, bf16[4,16,24,128]{3,2,1,0:T(8,128)(2,1)S(1)}, u32[]{:S(2)}, u32[]{:S(2)}) collective-permute-start(bf16[4,16,24,128]{3,2,1,0:T(8,128)(2,1)S(1)} %get-tuple-element.64), channel_id=1, source_target_pairs={{0,4},{4,0},{8,12},{12,8},{16,20},{20,16},{24,28},{28,24},{1,5},{5... | collective-permute-start | bytes 1179656 | tf_op jit(solution)/shard_map/ppermute | solution.py:349
  56.6 1.4 %gather_tiles.6 = (f32[4,16,24,128]{3,2,1,0:T(8,128)S(1)}, bf16[4,16,24,128]{3,2,1,0:T(8,128)(2,1)S(1)}) custom-call(s32[1,43]{1,0:T(1,128)S(1)} %copy-done.5, s32[1,43]{1,0:T(1,128)S(1)} %collective-permute-done.refs_1_, s32[1,43]{1,0:T(1,128)S(1)} %collective-permute-done.1.refs_2_, s32[1,43]{1,0:T(1,128)S(1)} %collective-permute-done.2.refs_3_, ...), custom_call_target="tpu_custom_call" | custom-call | flops 393216 | bytes 3145728 | tf_op jit(solution)/shard_map/gather_tiles/pallas_call | solution.py:225
  58.0 0.6 collective-permute-start.20
  58.6 0.9 collective-permute-done.25.refs_6_
  59.5 2.3 %collective-permute-done.26.refs_7_ = bf16[43,16,128]{2,1,0:T(8,128)(2,1)S(1)} collective-permute-done((bf16[43,16,128]{2,1,0:T(8,128)(2,1)}, bf16[43,16,128]{2,1,0:T(8,128)(2,1)S(1)}, u32[]{:S(2)}, u32[]{:S(2)}) %collective-permute-start.26) | collective-permute-done | bytes 176160 | tf_op jit(solution)/shard_map/ppermute | solution.py:346
  61.8 0.9 copy-done.3
  62.7 1.4 %gather_tiles.7 = (f32[4,16,16,128]{3,2,1,0:T(8,128)S(1)}, bf16[4,16,16,128]{3,2,1,0:T(8,128)(2,1)S(1)}) custom-call(s32[1,43]{1,0:T(1,128)S(1)} %copy-done.5, s32[1,43]{1,0:T(1,128)S(1)} %collective-permute-done.refs_1_, s32[1,43]{1,0:T(1,128)S(1)} %collective-permute-done.1.refs_2_, s32[1,43]{1,0:T(1,128)S(1)} %collective-permute-done.2.refs_3_, ...), custom_call_target="tpu_custom_call" | custom-call | flops 262144 | bytes 2097152 | tf_op jit(solution)/shard_map/gather_tiles/pallas_call | solution.py:225
  64.1 1.6 %collective-permute-start.27 = (bf16[4,16,16,128]{3,2,1,0:T(8,128)(2,1)S(1)}, bf16[4,16,16,128]{3,2,1,0:T(8,128)(2,1)S(1)}, u32[]{:S(2)}, u32[]{:S(2)}) collective-permute-start(bf16[4,16,16,128]{3,2,1,0:T(8,128)(2,1)S(1)} %get-tuple-element.84), channel_id=1, source_target_pairs={{0,4},{4,0},{8,12},{12,8},{16,20},{20,16},{24,28},{28,24},{1,5},{5... | collective-permute-start | bytes 786440 | tf_op jit(solution)/shard_map/ppermute | solution.py:349
  65.7 19.0 %collective-permute-done.27.refs_1_ = bf16[4,16,16,128]{3,2,1,0:T(8,128)(2,1)S(1)} collective-permute-done((bf16[4,16,16,128]{3,2,1,0:T(8,128)(2,1)S(1)}, bf16[4,16,16,128]{3,2,1,0:T(8,128)(2,1)S(1)}, u32[]{:S(2)}, u32[]{:S(2)}) %collective-permute-start.27) | collective-permute-done | bytes 262176 | tf_op jit(solution)/shard_map/ppermute | solution.py:349
  84.7 0.7 merge.7
  85.4 1.8 %collective-permute-start.28 = (bf16[1,16,16,128]{3,2,1,0:T(8,128)(2,1)S(1)}, bf16[1,16,16,128]{3,2,1,0:T(8,128)(2,1)S(1)}, u32[]{:S(2)}, u32[]{:S(2)}) collective-permute-start(bf16[1,16,16,128]{3,2,1,0:T(8,128)(2,1)S(1)} %get-tuple-element.86), channel_id=1, source_target_pairs={{0,8},{4,12},{8,0},{12,4},{16,24},{20,28},{24,16},{28,20},{1,9},{5... | collective-permute-start | bytes 196616 | tf_op jit(solution)/shard_map/ppermute | solution.py:349
  87.2 2.6 %collective-permute-start.29 = (bf16[1,16,16,128]{3,2,1,0:T(8,128)(2,1)S(1)}, bf16[1,16,16,128]{3,2,1,0:T(8,128)(2,1)S(1)}, u32[]{:S(2)}, u32[]{:S(2)}) collective-permute-start(bf16[1,16,16,128]{3,2,1,0:T(8,128)(2,1)S(1)} %get-tuple-element.87), channel_id=1, source_target_pairs={{0,16},{4,20},{8,24},{12,28},{16,0},{20,4},{24,8},{28,12},{1,17},{... | collective-permute-start | bytes 196616 | tf_op jit(solution)/shard_map/ppermute | solution.py:349
  89.8 0.7 merge.5
  90.5 0.5 collective-permute-start.14
  91.0 0.1 collective-permute-start.15
  91.1 0.7 merge.6
  91.8 3.8 %collective-permute-start.16 = (bf16[1,16,24,128]{3,2,1,0:T(8,128)(2,1)}, bf16[1,16,24,128]{3,2,1,0:T(8,128)(2,1)S(1)}, u32[]{:S(2)}, u32[]{:S(2)}) collective-permute-start(bf16[1,16,24,128]{3,2,1,0:T(8,128)(2,1)} %get-tuple-element.68), channel_id=1, source_target_pairs={{0,24},{4,28},{8,16},{12,20},{16,8},{20,12},{24,0},{28,4},{1,25},{... | collective-permute-start | bytes 294920 | tf_op jit(solution)/shard_map/ppermute | solution.py:349
  95.6 0.4 collective-permute-done.29
  96.0 1.6 %collective-permute-start.30 = (bf16[1,16,16,128]{3,2,1,0:T(8,128)(2,1)}, bf16[1,16,16,128]{3,2,1,0:T(8,128)(2,1)S(1)}, u32[]{:S(2)}, u32[]{:S(2)}) collective-permute-start(bf16[1,16,16,128]{3,2,1,0:T(8,128)(2,1)} %get-tuple-element.88), channel_id=1, source_target_pairs={{0,24},{4,28},{8,16},{12,20},{16,8},{20,12},{24,0},{28,4},{1,25},{... | collective-permute-start | bytes 196616 | tf_op jit(solution)/shard_map/ppermute | solution.py:349
  97.6 0.1 dynamic_slice.3
  97.7 0.1 merge.4
  97.7 4.6 %collective-permute-done.30 = bf16[1,16,16,128]{3,2,1,0:T(8,128)(2,1)S(1)} collective-permute-done((bf16[1,16,16,128]{3,2,1,0:T(8,128)(2,1)}, bf16[1,16,16,128]{3,2,1,0:T(8,128)(2,1)S(1)}, u32[]{:S(2)}, u32[]{:S(2)}) %collective-permute-start.30) | collective-permute-done | bytes 65568 | tf_op jit(solution)/shard_map/ppermute | solution.py:349
  102.4 2.5 %collective-permute-start.22 = (bf16[1,16,24,128]{3,2,1,0:T(8,128)(2,1)S(1)}, bf16[1,16,24,128]{3,2,1,0:T(8,128)(2,1)S(1)}, u32[]{:S(2)}, u32[]{:S(2)}) collective-permute-start(bf16[1,16,24,128]{3,2,1,0:T(8,128)(2,1)S(1)} %get-tuple-element.77), channel_id=1, source_target_pairs={{0,16},{4,20},{8,24},{12,28},{16,0},{20,4},{24,8},{28,12},{1,17},{... | collective-permute-start | bytes 294920 | tf_op jit(solution)/shard_map/ppermute | solution.py:349
  104.8 2.5 %collective-permute-start.23 = (bf16[1,16,24,128]{3,2,1,0:T(8,128)(2,1)S(1)}, bf16[1,16,24,128]{3,2,1,0:T(8,128)(2,1)S(1)}, u32[]{:S(2)}, u32[]{:S(2)}) collective-permute-start(bf16[1,16,24,128]{3,2,1,0:T(8,128)(2,1)S(1)} %get-tuple-element.78), channel_id=1, source_target_pairs={{0,24},{4,28},{8,16},{12,20},{16,8},{20,12},{24,0},{28,4},{1,25},{... | collective-permute-start | bytes 294920 | tf_op jit(solution)/shard_map/ppermute | solution.py:349
  107.4 1.9 %collective-permute-start.8 = (bf16[1,16,32,128]{3,2,1,0:T(8,128)(2,1)S(1)}, bf16[1,16,32,128]{3,2,1,0:T(8,128)(2,1)S(1)}, u32[]{:S(2)}, u32[]{:S(2)}) collective-permute-start(bf16[1,16,32,128]{3,2,1,0:T(8,128)(2,1)S(1)} %get-tuple-element.56), channel_id=1, source_target_pairs={{0,16},{4,20},{8,24},{12,28},{16,0},{20,4},{24,8},{28,12},{1,17},{... | collective-permute-start | bytes 393224 | tf_op jit(solution)/shard_map/ppermute | solution.py:349
  109.2 2.5 %collective-permute-start.9 = (bf16[1,16,32,128]{3,2,1,0:T(8,128)(2,1)S(1)}, bf16[1,16,32,128]{3,2,1,0:T(8,128)(2,1)S(1)}, u32[]{:S(2)}, u32[]{:S(2)}) collective-permute-start(bf16[1,16,32,128]{3,2,1,0:T(8,128)(2,1)S(1)} %get-tuple-element.57), channel_id=1, source_target_pairs={{0,24},{4,28},{8,16},{12,20},{16,8},{20,12},{24,0},{28,4},{1,25},{... | collective-permute-start | bytes 393224 | tf_op jit(solution)/shard_map/ppermute | solution.py:349
  111.7 0.1 fusion
  111.8 0.1 copy.10.refs_0_
  111.9 0.1 reshape.37.refs_2_
  112.0 2.5 %collective-permute-done.22 = bf16[1,16,24,128]{3,2,1,0:T(8,128)(2,1)S(1)} collective-permute-done((bf16[1,16,24,128]{3,2,1,0:T(8,128)(2,1)S(1)}, bf16[1,16,24,128]{3,2,1,0:T(8,128)(2,1)S(1)}, u32[]{:S(2)}, u32[]{:S(2)}) %collective-permute-start.22) | collective-permute-done | bytes 98336 | tf_op jit(solution)/shard_map/ppermute | solution.py:349
  114.5 1.2 collective-permute-done.7
  115.6 7.2 %collective-permute-done.8 = bf16[1,16,32,128]{3,2,1,0:T(8,128)(2,1)S(1)} collective-permute-done((bf16[1,16,32,128]{3,2,1,0:T(8,128)(2,1)S(1)}, bf16[1,16,32,128]{3,2,1,0:T(8,128)(2,1)S(1)}, u32[]{:S(2)}, u32[]{:S(2)}) %collective-permute-start.8) | collective-permute-done | bytes 131104 | tf_op jit(solution)/shard_map/ppermute | solution.py:349
  122.9 1.4 %finish.1 = bf16[64,3072]{1,0:T(8,128)(2,1)} custom-call(f32[64,1]{1,0:T(8,128)S(1)} %copy.10.refs_0_, f32[1,3072]{1,0:T(1,128)S(1)} %bitcast.38, s32[1,3072]{1,0:T(1,128)S(1)} %reshape.37.refs_2_, f32[16,32,128]{2,1,0:T(8,128)S(1)} %bitcast.22, bf16[16,32,128]{2,1,0:T(8,128)(2,1)S(1)} %bitcast.26, bf16[16,32,128]{2,1,0:T(8,128)(2,1)S(1)} %bitcast.27, ...), custom_call_target="tpu_custom_call" | custom-call | tf_op jit(solution)/shard_map/finish/pallas_call | solution.py:303
  (37 shorter events, 0.1 us)
Async XLA Ops:
  4.9 7.5 %copy-start.5 = (s32[1,43]{1,0:T(1,128)S(1)}, s32[1,43]{1,0:T(1,128)}, u32[]{:S(2)}) copy-start(s32[1,43]{1,0:T(1,128)} %get-tuple-element.47.refs_0_) | copy-start | bytes 520
  4.9 20.3 %copy-start.10 = (bf16[43,32,128]{2,1,0:T(8,128)(2,1)S(1)}, bf16[43,32,128]{2,1,0:T(8,128)(2,1)}, u32[]{:S(2)}) copy-start(bf16[43,32,128]{2,1,0:T(8,128)(2,1)} %get-tuple-element.49) | copy-start | bytes 1056772
  4.9 20.8 %copy-start.9 = (bf16[43,32,128]{2,1,0:T(8,128)(2,1)S(1)}, bf16[43,32,128]{2,1,0:T(8,128)(2,1)}, u32[]{:S(2)}) copy-start(bf16[43,32,128]{2,1,0:T(8,128)(2,1)} %get-tuple-element.50) | copy-start | bytes 1056772
  4.9 22.6 %copy-start.8 = (bf16[43,32,128]{2,1,0:T(8,128)(2,1)S(1)}, bf16[43,32,128]{2,1,0:T(8,128)(2,1)}, u32[]{:S(2)}) copy-start(bf16[43,32,128]{2,1,0:T(8,128)(2,1)} %get-tuple-element.51) | copy-start | bytes 1056772
  9.3 16.5 %collective-permute-start.10 = (bf16[43,24,128]{2,1,0:T(8,128)(2,1)}, bf16[43,24,128]{2,1,0:T(8,128)(2,1)S(1)}, u32[]{:S(2)}, u32[]{:S(2)}) collective-permute-start(bf16[43,24,128]{2,1,0:T(8,128)(2,1)} %get-tuple-element.60), channel_id=1, source_target_pairs={{0,1},{1,0},{2,3},{3,2},{4,5},{5,4},{6,7},{7,6},{8,9},{9,8},{10,11... | collective-permute-start | bytes 792584 | tf_op jit(solution)/shard_map/ppermute | solution.py:346
  9.8 17.7 %collective-permute-start.11 = (bf16[43,24,128]{2,1,0:T(8,128)(2,1)}, bf16[43,24,128]{2,1,0:T(8,128)(2,1)S(1)}, u32[]{:S(2)}, u32[]{:S(2)}) collective-permute-start(bf16[43,24,128]{2,1,0:T(8,128)(2,1)} %get-tuple-element.61), channel_id=1, source_target_pairs={{0,2},{1,3},{2,0},{3,1},{4,6},{5,7},{6,4},{7,5},{8,10},{9,11},{10,... | collective-permute-start | bytes 792584 | tf_op jit(solution)/shard_map/ppermute | solution.py:346
  12.4 15.1 %collective-permute-start.12 = (bf16[43,24,128]{2,1,0:T(8,128)(2,1)}, bf16[43,24,128]{2,1,0:T(8,128)(2,1)S(1)}, u32[]{:S(2)}, u32[]{:S(2)}) collective-permute-start(bf16[43,24,128]{2,1,0:T(8,128)(2,1)} %get-tuple-element.62), channel_id=1, source_target_pairs={{0,3},{1,2},{2,1},{3,0},{4,7},{5,6},{6,5},{7,4},{8,11},{9,10},{10,... | collective-permute-start | bytes 792584 | tf_op jit(solution)/shard_map/ppermute | solution.py:346
  12.4 33.1 %copy-start = (bf16[43,32,128]{2,1,0:T(8,128)(2,1)S(1)}, bf16[43,32,128]{2,1,0:T(8,128)(2,1)}, u32[]{:S(2)}) copy-start(bf16[43,32,128]{2,1,0:T(8,128)(2,1)} %get-tuple-element.48.refs_4_) | copy-start | bytes 1056772
  12.4 39.3 %copy-start.1 = (bf16[43,24,128]{2,1,0:T(8,128)(2,1)S(1)}, bf16[43,24,128]{2,1,0:T(8,128)(2,1)}, u32[]{:S(2)}) copy-start(bf16[43,24,128]{2,1,0:T(8,128)(2,1)} %get-tuple-element.59.refs_4_) | copy-start | bytes 792580
  12.4 6.4 %collective-permute-start = (s32[1,43]{1,0:T(1,128)S(1)}, s32[1,43]{1,0:T(1,128)S(1)}, u32[]{:S(2)}, u32[]{:S(2)}) collective-permute-start(s32[1,43]{1,0:T(1,128)S(1)} %copy-done.5), channel_id=1, source_target_pairs={{0,1},{1,0},{2,3},{3,2},{4,5},{5,4},{6,7},{7,6},{8,9},{9,8},{10,11... | collective-permute-start | bytes 524 | tf_op jit(solution)/shard_map/ppermute | solution.py:346
  12.6 12.6 %collective-permute-start.1 = (s32[1,43]{1,0:T(1,128)S(1)}, s32[1,43]{1,0:T(1,128)S(1)}, u32[]{:S(2)}, u32[]{:S(2)}) collective-permute-start(s32[1,43]{1,0:T(1,128)S(1)} %copy-done.5), channel_id=1, source_target_pairs={{0,2},{1,3},{2,0},{3,1},{4,6},{5,7},{6,4},{7,5},{8,10},{9,11},{10,... | collective-permute-start | bytes 524 | tf_op jit(solution)/shard_map/ppermute | solution.py:346
  18.8 37.8 %copy-start.2 = (bf16[43,24,128]{2,1,0:T(8,128)(2,1)S(1)}, bf16[43,24,128]{2,1,0:T(8,128)(2,1)}, u32[]{:S(2)}) copy-start(bf16[43,24,128]{2,1,0:T(8,128)(2,1)} %get-tuple-element.69.refs_4_) | copy-start | bytes 792580
  18.8 78.8 %copy-start.6 = (s32[128]{0:T(128)S(1)}, s32[128]{0:T(128)}, u32[]{:S(2)}) copy-start(s32[128]{0:T(128)} %refs_3_.1) | copy-start | bytes 1540
  18.8 93.0 %copy-start.7 = (f32[64]{0:T(128)S(1)}, f32[64]{0:T(128)}, u32[]{:S(2)}) copy-start(f32[64]{0:T(128)} %param.16) | copy-start | bytes 772
  18.8 104.0 %copy-start.4 = (f32[3072]{0:T(1024)S(1)}, f32[3072]{0:T(1024)}, u32[]{:S(2)}) copy-start(f32[3072]{0:T(1024)} %param.17) | copy-start | bytes 36868
  18.8 6.4 %collective-permute-start.2 = (s32[1,43]{1,0:T(1,128)S(1)}, s32[1,43]{1,0:T(1,128)S(1)}, u32[]{:S(2)}, u32[]{:S(2)}) collective-permute-start(s32[1,43]{1,0:T(1,128)S(1)} %copy-done.5), channel_id=1, source_target_pairs={{0,3},{1,2},{2,1},{3,0},{4,7},{5,6},{6,5},{7,4},{8,11},{9,10},{10,... | collective-permute-start | bytes 524 | tf_op jit(solution)/shard_map/ppermute | solution.py:346
  25.2 3.7 %collective-permute-start.17 = (bf16[43,24,128]{2,1,0:T(8,128)(2,1)}, bf16[43,24,128]{2,1,0:T(8,128)(2,1)S(1)}, u32[]{:S(2)}, u32[]{:S(2)}) collective-permute-start(bf16[43,24,128]{2,1,0:T(8,128)(2,1)} %get-tuple-element.70), channel_id=1, source_target_pairs={{0,1},{1,0},{2,3},{3,2},{4,5},{5,4},{6,7},{7,6},{8,9},{9,8},{10,11... | collective-permute-start | bytes 792584 | tf_op jit(solution)/shard_map/ppermute | solution.py:346
  25.2 7.6 %collective-permute-start.3 = (bf16[43,32,128]{2,1,0:T(8,128)(2,1)S(1)}, bf16[43,32,128]{2,1,0:T(8,128)(2,1)S(1)}, u32[]{:S(2)}, u32[]{:S(2)}) collective-permute-start(bf16[43,32,128]{2,1,0:T(8,128)(2,1)S(1)} %copy-done.10), channel_id=1, source_target_pairs={{0,1},{1,0},{2,3},{3,2},{4,5},{5,4},{6,7},{7,6},{8,9},{9,8},{10,11... | collective-permute-start | bytes 1056776 | tf_op jit(solution)/shard_map/ppermute | solution.py:346
  25.8 11.1 %collective-permute-start.4 = (bf16[43,32,128]{2,1,0:T(8,128)(2,1)S(1)}, bf16[43,32,128]{2,1,0:T(8,128)(2,1)S(1)}, u32[]{:S(2)}, u32[]{:S(2)}) collective-permute-start(bf16[43,32,128]{2,1,0:T(8,128)(2,1)S(1)} %copy-done.9), channel_id=1, source_target_pairs={{0,2},{1,3},{2,0},{3,1},{4,6},{5,7},{6,4},{7,5},{8,10},{9,11},{10,... | collective-permute-start | bytes 1056776 | tf_op jit(solution)/shard_map/ppermute | solution.py:346
  27.5 16.2 %collective-permute-start.5 = (bf16[43,32,128]{2,1,0:T(8,128)(2,1)S(1)}, bf16[43,32,128]{2,1,0:T(8,128)(2,1)S(1)}, u32[]{:S(2)}, u32[]{:S(2)}) collective-permute-start(bf16[43,32,128]{2,1,0:T(8,128)(2,1)S(1)} %copy-done.8), channel_id=1, source_target_pairs={{0,3},{1,2},{2,1},{3,0},{4,7},{5,6},{6,5},{7,4},{8,11},{9,10},{10,... | collective-permute-start | bytes 1056776 | tf_op jit(solution)/shard_map/ppermute | solution.py:346
  27.5 22.6 %collective-permute-start.18 = (bf16[43,24,128]{2,1,0:T(8,128)(2,1)}, bf16[43,24,128]{2,1,0:T(8,128)(2,1)S(1)}, u32[]{:S(2)}, u32[]{:S(2)}) collective-permute-start(bf16[43,24,128]{2,1,0:T(8,128)(2,1)} %get-tuple-element.71), channel_id=1, source_target_pairs={{0,2},{1,3},{2,0},{3,1},{4,6},{5,7},{6,4},{7,5},{8,10},{9,11},{10,... | collective-permute-start | bytes 792584 | tf_op jit(solution)/shard_map/ppermute | solution.py:346
  28.9 26.2 %collective-permute-start.19 = (bf16[43,24,128]{2,1,0:T(8,128)(2,1)}, bf16[43,24,128]{2,1,0:T(8,128)(2,1)S(1)}, u32[]{:S(2)}, u32[]{:S(2)}) collective-permute-start(bf16[43,24,128]{2,1,0:T(8,128)(2,1)} %get-tuple-element.72), channel_id=1, source_target_pairs={{0,3},{1,2},{2,1},{3,0},{4,7},{5,6},{6,5},{7,4},{8,11},{9,10},{10,... | collective-permute-start | bytes 792584 | tf_op jit(solution)/shard_map/ppermute | solution.py:346
  32.8 25.1 %collective-permute-start.24 = (bf16[43,16,128]{2,1,0:T(8,128)(2,1)}, bf16[43,16,128]{2,1,0:T(8,128)(2,1)S(1)}, u32[]{:S(2)}, u32[]{:S(2)}) collective-permute-start(bf16[43,16,128]{2,1,0:T(8,128)(2,1)} %get-tuple-element.80), channel_id=1, source_target_pairs={{0,1},{1,0},{2,3},{3,2},{4,5},{5,4},{6,7},{7,6},{8,9},{9,8},{10,11... | collective-permute-start | bytes 528392 | tf_op jit(solution)/shard_map/ppermute | solution.py:346
  36.9 22.6 %collective-permute-start.25 = (bf16[43,16,128]{2,1,0:T(8,128)(2,1)}, bf16[43,16,128]{2,1,0:T(8,128)(2,1)S(1)}, u32[]{:S(2)}, u32[]{:S(2)}) collective-permute-start(bf16[43,16,128]{2,1,0:T(8,128)(2,1)} %get-tuple-element.81), channel_id=1, source_target_pairs={{0,2},{1,3},{2,0},{3,1},{4,6},{5,7},{6,4},{7,5},{8,10},{9,11},{10,... | collective-permute-start | bytes 528392 | tf_op jit(solution)/shard_map/ppermute | solution.py:346
  43.7 18.1 %collective-permute-start.26 = (bf16[43,16,128]{2,1,0:T(8,128)(2,1)}, bf16[43,16,128]{2,1,0:T(8,128)(2,1)S(1)}, u32[]{:S(2)}, u32[]{:S(2)}) collective-permute-start(bf16[43,16,128]{2,1,0:T(8,128)(2,1)} %get-tuple-element.82), channel_id=1, source_target_pairs={{0,3},{1,2},{2,1},{3,0},{4,7},{5,6},{6,5},{7,4},{8,11},{9,10},{10,... | collective-permute-start | bytes 528392 | tf_op jit(solution)/shard_map/ppermute | solution.py:346
  50.1 45.9 %collective-permute-start.6 = (bf16[4,16,32,128]{3,2,1,0:T(8,128)(2,1)S(1)}, bf16[4,16,32,128]{3,2,1,0:T(8,128)(2,1)S(1)}, u32[]{:S(2)}, u32[]{:S(2)}) collective-permute-start(bf16[4,16,32,128]{3,2,1,0:T(8,128)(2,1)S(1)} %get-tuple-element.53), channel_id=1, source_target_pairs={{0,4},{4,0},{8,12},{12,8},{16,20},{20,16},{24,28},{28,24},{1,5},{5... | collective-permute-start | bytes 1572872 | tf_op jit(solution)/shard_map/ppermute | solution.py:349
  55.1 34.7 %collective-permute-start.13 = (bf16[4,16,24,128]{3,2,1,0:T(8,128)(2,1)S(1)}, bf16[4,16,24,128]{3,2,1,0:T(8,128)(2,1)S(1)}, u32[]{:S(2)}, u32[]{:S(2)}) collective-permute-start(bf16[4,16,24,128]{3,2,1,0:T(8,128)(2,1)S(1)} %get-tuple-element.64), channel_id=1, source_target_pairs={{0,4},{4,0},{8,12},{12,8},{16,20},{20,16},{24,28},{28,24},{1,5},{5... | collective-permute-start | bytes 1179656 | tf_op jit(solution)/shard_map/ppermute | solution.py:349
  58.0 33.0 %collective-permute-start.20 = (bf16[4,16,24,128]{3,2,1,0:T(8,128)(2,1)S(1)}, bf16[4,16,24,128]{3,2,1,0:T(8,128)(2,1)S(1)}, u32[]{:S(2)}, u32[]{:S(2)}) collective-permute-start(bf16[4,16,24,128]{3,2,1,0:T(8,128)(2,1)S(1)} %get-tuple-element.74), channel_id=1, source_target_pairs={{0,4},{4,0},{8,12},{12,8},{16,20},{20,16},{24,28},{28,24},{1,5},{5... | collective-permute-start | bytes 1179656 | tf_op jit(solution)/shard_map/ppermute | solution.py:349
  61.8 0.9 copy-start.3
  64.1 20.6 %collective-permute-start.27 = (bf16[4,16,16,128]{3,2,1,0:T(8,128)(2,1)S(1)}, bf16[4,16,16,128]{3,2,1,0:T(8,128)(2,1)S(1)}, u32[]{:S(2)}, u32[]{:S(2)}) collective-permute-start(bf16[4,16,16,128]{3,2,1,0:T(8,128)(2,1)S(1)} %get-tuple-element.84), channel_id=1, source_target_pairs={{0,4},{4,0},{8,12},{12,8},{16,20},{20,16},{24,28},{28,24},{1,5},{5... | collective-permute-start | bytes 786440 | tf_op jit(solution)/shard_map/ppermute | solution.py:349
  85.4 6.4 %collective-permute-start.28 = (bf16[1,16,16,128]{3,2,1,0:T(8,128)(2,1)S(1)}, bf16[1,16,16,128]{3,2,1,0:T(8,128)(2,1)S(1)}, u32[]{:S(2)}, u32[]{:S(2)}) collective-permute-start(bf16[1,16,16,128]{3,2,1,0:T(8,128)(2,1)S(1)} %get-tuple-element.86), channel_id=1, source_target_pairs={{0,8},{4,12},{8,0},{12,4},{16,24},{20,28},{24,16},{28,20},{1,9},{5... | collective-permute-start | bytes 196616 | tf_op jit(solution)/shard_map/ppermute | solution.py:349
  87.2 8.8 %collective-permute-start.29 = (bf16[1,16,16,128]{3,2,1,0:T(8,128)(2,1)S(1)}, bf16[1,16,16,128]{3,2,1,0:T(8,128)(2,1)S(1)}, u32[]{:S(2)}, u32[]{:S(2)}) collective-permute-start(bf16[1,16,16,128]{3,2,1,0:T(8,128)(2,1)S(1)} %get-tuple-element.87), channel_id=1, source_target_pairs={{0,16},{4,20},{8,24},{12,28},{16,0},{20,4},{24,8},{28,12},{1,17},{... | collective-permute-start | bytes 196616 | tf_op jit(solution)/shard_map/ppermute | solution.py:349
  90.5 14.3 %collective-permute-start.14 = (bf16[1,16,24,128]{3,2,1,0:T(8,128)(2,1)}, bf16[1,16,24,128]{3,2,1,0:T(8,128)(2,1)S(1)}, u32[]{:S(2)}, u32[]{:S(2)}) collective-permute-start(bf16[1,16,24,128]{3,2,1,0:T(8,128)(2,1)} %get-tuple-element.66), channel_id=1, source_target_pairs={{0,8},{4,12},{8,0},{12,4},{16,24},{20,28},{24,16},{28,20},{1,9},{5... | collective-permute-start | bytes 294920 | tf_op jit(solution)/shard_map/ppermute | solution.py:349
  91.0 16.4 %collective-permute-start.15 = (bf16[1,16,24,128]{3,2,1,0:T(8,128)(2,1)}, bf16[1,16,24,128]{3,2,1,0:T(8,128)(2,1)S(1)}, u32[]{:S(2)}, u32[]{:S(2)}) collective-permute-start(bf16[1,16,24,128]{3,2,1,0:T(8,128)(2,1)} %get-tuple-element.67), channel_id=1, source_target_pairs={{0,16},{4,20},{8,24},{12,28},{16,0},{20,4},{24,8},{28,12},{1,17},{... | collective-permute-start | bytes 294920 | tf_op jit(solution)/shard_map/ppermute | solution.py:349
  91.8 15.6 %collective-permute-start.16 = (bf16[1,16,24,128]{3,2,1,0:T(8,128)(2,1)}, bf16[1,16,24,128]{3,2,1,0:T(8,128)(2,1)S(1)}, u32[]{:S(2)}, u32[]{:S(2)}) collective-permute-start(bf16[1,16,24,128]{3,2,1,0:T(8,128)(2,1)} %get-tuple-element.68), channel_id=1, source_target_pairs={{0,24},{4,28},{8,16},{12,20},{16,8},{20,12},{24,0},{28,4},{1,25},{... | collective-permute-start | bytes 294920 | tf_op jit(solution)/shard_map/ppermute | solution.py:349
  96.0 13.3 %collective-permute-start.21 = (bf16[1,16,24,128]{3,2,1,0:T(8,128)(2,1)}, bf16[1,16,24,128]{3,2,1,0:T(8,128)(2,1)S(1)}, u32[]{:S(2)}, u32[]{:S(2)}) collective-permute-start(bf16[1,16,24,128]{3,2,1,0:T(8,128)(2,1)} %get-tuple-element.76), channel_id=1, source_target_pairs={{0,8},{4,12},{8,0},{12,4},{16,24},{20,28},{24,16},{28,20},{1,9},{5... | collective-permute-start | bytes 294920 | tf_op jit(solution)/shard_map/ppermute | solution.py:349
  96.0 6.4 %collective-permute-start.30 = (bf16[1,16,16,128]{3,2,1,0:T(8,128)(2,1)}, bf16[1,16,16,128]{3,2,1,0:T(8,128)(2,1)S(1)}, u32[]{:S(2)}, u32[]{:S(2)}) collective-permute-start(bf16[1,16,16,128]{3,2,1,0:T(8,128)(2,1)} %get-tuple-element.88), channel_id=1, source_target_pairs={{0,24},{4,28},{8,16},{12,20},{16,8},{20,12},{24,0},{28,4},{1,25},{... | collective-permute-start | bytes 196616 | tf_op jit(solution)/shard_map/ppermute | solution.py:349
  102.4 12.1 %collective-permute-start.22 = (bf16[1,16,24,128]{3,2,1,0:T(8,128)(2,1)S(1)}, bf16[1,16,24,128]{3,2,1,0:T(8,128)(2,1)S(1)}, u32[]{:S(2)}, u32[]{:S(2)}) collective-permute-start(bf16[1,16,24,128]{3,2,1,0:T(8,128)(2,1)S(1)} %get-tuple-element.77), channel_id=1, source_target_pairs={{0,16},{4,20},{8,24},{12,28},{16,0},{20,4},{24,8},{28,12},{1,17},{... | collective-permute-start | bytes 294920 | tf_op jit(solution)/shard_map/ppermute | solution.py:349
  104.8 9.7 %collective-permute-start.23 = (bf16[1,16,24,128]{3,2,1,0:T(8,128)(2,1)S(1)}, bf16[1,16,24,128]{3,2,1,0:T(8,128)(2,1)S(1)}, u32[]{:S(2)}, u32[]{:S(2)}) collective-permute-start(bf16[1,16,24,128]{3,2,1,0:T(8,128)(2,1)S(1)} %get-tuple-element.78), channel_id=1, source_target_pairs={{0,24},{4,28},{8,16},{12,20},{16,8},{20,12},{24,0},{28,4},{1,25},{... | collective-permute-start | bytes 294920 | tf_op jit(solution)/shard_map/ppermute | solution.py:349
  107.4 8.3 %collective-permute-start.7 = (bf16[1,16,32,128]{3,2,1,0:T(8,128)(2,1)S(1)}, bf16[1,16,32,128]{3,2,1,0:T(8,128)(2,1)S(1)}, u32[]{:S(2)}, u32[]{:S(2)}) collective-permute-start(bf16[1,16,32,128]{3,2,1,0:T(8,128)(2,1)S(1)} %get-tuple-element.55), channel_id=1, source_target_pairs={{0,8},{4,12},{8,0},{12,4},{16,24},{20,28},{24,16},{28,20},{1,9},{5... | collective-permute-start | bytes 393224 | tf_op jit(solution)/shard_map/ppermute | solution.py:349
  107.4 15.5 %collective-permute-start.8 = (bf16[1,16,32,128]{3,2,1,0:T(8,128)(2,1)S(1)}, bf16[1,16,32,128]{3,2,1,0:T(8,128)(2,1)S(1)}, u32[]{:S(2)}, u32[]{:S(2)}) collective-permute-start(bf16[1,16,32,128]{3,2,1,0:T(8,128)(2,1)S(1)} %get-tuple-element.56), channel_id=1, source_target_pairs={{0,16},{4,20},{8,24},{12,28},{16,0},{20,4},{24,8},{28,12},{1,17},{... | collective-permute-start | bytes 393224 | tf_op jit(solution)/shard_map/ppermute | solution.py:349
  109.2 13.6 %collective-permute-start.9 = (bf16[1,16,32,128]{3,2,1,0:T(8,128)(2,1)S(1)}, bf16[1,16,32,128]{3,2,1,0:T(8,128)(2,1)S(1)}, u32[]{:S(2)}, u32[]{:S(2)}) collective-permute-start(bf16[1,16,32,128]{3,2,1,0:T(8,128)(2,1)S(1)} %get-tuple-element.57), channel_id=1, source_target_pairs={{0,24},{4,28},{8,16},{12,20},{16,8},{20,12},{24,0},{28,4},{1,25},{... | collective-permute-start | bytes 393224 | tf_op jit(solution)/shard_map/ppermute | solution.py:349
